TPU v7x, 512 devices: a whole 4x4x16 slice. The times are simulated.
512 devices in a mesh: scen: 16 (over x, y_hi, core), blk: 32 (over y_lo, z).
Axes of the slice: x: 4, y: 4 (y_hi: 2, y_lo: 2; y = y_hi * 2 + y_lo), z: 16, core: 2. Of those that a mesh axis runs over, the one named last changes fastest.
Arguments:
- blocks: bfloat16 [512, 20, 128, 128], P(('scen', 'blk')), parts along dimension 0, may hold values from -0.125 to 0.125
- col_index: int32 [512, 20], P(('scen', 'blk')), parts along dimension 0, may hold values from 0 to 127, as said below
- cost: float32 [262144], P(('scen', 'blk')), parts along dimension 0, may hold values from -6 to 6
- upper: float32 [262144], P(('scen', 'blk')), parts along dimension 0, may hold values from 0.5 to 1.5
- capacity: float32 [65536], P(('scen', 'blk')), parts along dimension 0, may hold values from 0.5 to 2
- disrupted: int32 [1024, 4096], P('scen', 'blk'), parts along dimension 0, may hold values 0 or 1
- x_start: float32 [1024, 16384], P('scen', 'blk'), parts along dimension 0, may hold values from 0 to 1
- y_start: float32 [1024, 4096], P('scen', 'blk'), parts along dimension 0, may hold values from 0 to 1
Outputs:
- x_final: float32 [1024, 16384], P('scen', 'blk'), parts along dimension 0
- y_final: float32 [1024, 4096], P('scen', 'blk'), parts along dimension 0
There are 16 independent parts, one for each index of `scen`. A program takes and returns all parts, laid end to end along the dimension named above; each array names one. Nothing has to cross between parts.
Inputs may be any that keep to these rules, and one draw needn't show every extreme that they name: `col_index`: with row block r on band device b = r, slot n lies on device (b + n // 4 - 2) modulo the number of devices along the band, that is, its value is that device times 4 plus some column block of it; the first row block of every device takes that device's first column block in slot position 0 and its last in position 1 of each group of 4.
All inputs are finite; a program needn't handle non-finite values. No bound on the sum of `disrupted` on one device may be relied on, other than what follows from the above.
Results may differ from a plain program's by a relative error of at most 0.0025.
Values may be sent and summed in bfloat16 or wider, within the bound.
A program may use at most 64 MiB of HBM per device.

v0:
```python
import jax
import jax.numpy as jnp
from jax import lax
from jax.sharding import PartitionSpec as P

REACH = 2
ITERS = 4


step_primal = 0.4
step_dual = 0.4


def shifted(value, axis, steps):
    count = lax.axis_size(axis)
    pairs = [(source, (source + steps) % count) for source in range(count)]
    return lax.ppermute(value, axis, pairs)


def collect_band_rows(own):
    pieces = {0: own}
    for offset in range(-REACH, REACH + 1):
        if offset != 0:
            pieces[offset] = shifted(own, "blk", -offset)
    return jnp.concatenate([pieces[offset] for offset in range(-REACH, REACH + 1)], axis=1)


def return_terms(spread, col_blocks):

    def part_of(offset):
        start = (offset + REACH) * col_blocks
        return spread[start : start + col_blocks]

    total = part_of(0)
    for offset in range(-REACH, REACH + 1):
        if offset != 0:
            total = total + shifted(part_of(offset), "blk", offset)
    return total


def per_device(blocks, col_index, cost, upper, capacity, disrupted, x_start, y_start):
    width = blocks.shape[-1]
    rows_here = blocks.shape[0]
    slots = blocks.shape[1]
    scen = x_start.shape[0]
    col_blocks = x_start.shape[1] // width
    groups = 2 * REACH + 1
    bound = capacity[None, :] * jnp.where(disrupted == 1, 0.25, 1.0)
    primal = x_start
    dual = y_start
    n_dev = lax.axis_size("blk")
    me_index = lax.axis_index("blk")
    owner = col_index // col_blocks
    offset_map = (owner - me_index) % n_dev
    offset_map = jnp.where(offset_map > n_dev // 2, offset_map - n_dev, offset_map)
    local = ((offset_map + REACH) * col_blocks + col_index % col_blocks).reshape(-1)
    spans = groups * col_blocks
    for step in range(ITERS):
        dual_lower_part = dual.astype(jnp.bfloat16).reshape(scen, rows_here, width)
        partial_terms = jnp.einsum(
            "aqd,qudk->quak", dual_lower_part, blocks, preferred_element_type=jnp.float32
        )
        partial_terms = partial_terms.reshape(rows_here * slots, scen, width)
        spread = jax.ops.segment_sum(partial_terms, local, num_segments=spans)
        summed = return_terms(spread, col_blocks)
        pull = cost[None, :] + jnp.transpose(summed, (1, 0, 2)).reshape(scen, col_blocks * width)
        x_new = jnp.minimum(jnp.maximum(primal - step_primal * pull, 0.0), upper[None, :])
        x_bar = (2.0 * x_new - primal).astype(jnp.bfloat16).reshape(scen, col_blocks, width)
        window = collect_band_rows(x_bar)
        selected_entries = jnp.take(window, local, axis=1).reshape(scen, rows_here, slots, width)
        mapped_output = jnp.einsum(
            "ufol,foql->ufq", selected_entries, blocks, preferred_element_type=jnp.float32
        )
        mapped_output = mapped_output.reshape(scen, rows_here * width)
        dual = jnp.maximum(dual + step_dual * (mapped_output - bound), 0.0)
        primal = x_new
    return (primal, dual)


def solution(mesh):
    placed = (
        P(("scen", "blk"), None, None, None),
        P(("scen", "blk"), None),
        P(("scen", "blk")),
        P(("scen", "blk")),
        P(("scen", "blk")),
        P("scen", "blk"),
        P("scen", "blk"),
        P("scen", "blk"),
    )
    return jax.shard_map(
        per_device,
        mesh=mesh,
        in_specs=placed,
        out_specs=(P("scen", "blk"), P("scen", "blk")),
        check_vma=False,
    )
```

profile of v0, /device:TPU:6, one launch (start us, length us, event | category | flops | bytes accessed | tf_op | source)
XLA Modules:
  0.0 187.8 jit_solution(5631574823915820195)
XLA Ops:
  2.8 2.3 %scatter_fusion = f32[20,64,128]{2,1,0:T(8,128)S(1)} fusion(f32[20,64,128]{2,1,0:T(8,128)S(1)} %broadcast.63.clone.1, s32[20]{0:T(128)S(1)} %get-tuple-element.8, f32[20,64,128]{2,1,0:T(8,128)S(1)} %convolution_bitcast_fusion), kind=kCustom, calls=%fused_computation.4 | custom fusion | flops 163840 | bytes 1966160 | tf_op jit(solution)/shard_map/scatter-add | solution.py:64
  5.2 13.0 %collective-permute-start = (f32[4,64,128]{2,1,0:T(8,128)S(1)}, f32[4,64,128]{2,1,0:T(8,128)S(1)}, u32[]{:S(2)}, u32[]{:S(2)}) collective-permute-start(f32[4,64,128]{2,1,0:T(8,128)S(1)} %get-tuple-element.21), channel_id=1, source_target_pairs={{0,30},{1,31},{2,0},{3,1},{4,2},{5,3},{6,4},{7,5},{8,6},{9,7},{10,... | collective-permute-start | bytes 393224 | tf_op jit(solution)/shard_map/ppermute | solution.py:17
  18.2 2.9 %collective-permute-start.1 = (f32[4,64,128]{2,1,0:T(8,128)S(1)}, f32[4,64,128]{2,1,0:T(8,128)S(1)}, u32[]{:S(2)}, u32[]{:S(2)}) collective-permute-start(f32[4,64,128]{2,1,0:T(8,128)S(1)} %get-tuple-element.24), channel_id=1, source_target_pairs={{0,31},{1,0},{2,1},{3,2},{4,3},{5,4},{6,5},{7,6},{8,7},{9,8},{10,9... | collective-permute-start | bytes 393224 | tf_op jit(solution)/shard_map/ppermute | solution.py:17
  21.1 2.9 %collective-permute-start.2 = (f32[4,64,128]{2,1,0:T(8,128)S(1)}, f32[4,64,128]{2,1,0:T(8,128)S(1)}, u32[]{:S(2)}, u32[]{:S(2)}) collective-permute-start(f32[4,64,128]{2,1,0:T(8,128)S(1)} %get-tuple-element.23), channel_id=1, source_target_pairs={{0,1},{1,2},{2,3},{3,4},{4,5},{5,6},{6,7},{7,8},{8,9},{9,10},{10,1... | collective-permute-start | bytes 393224 | tf_op jit(solution)/shard_map/ppermute | solution.py:17
  24.0 2.4 %collective-permute-start.3 = (f32[4,64,128]{2,1,0:T(8,128)S(1)}, f32[4,64,128]{2,1,0:T(8,128)S(1)}, u32[]{:S(2)}, u32[]{:S(2)}) collective-permute-start(f32[4,64,128]{2,1,0:T(8,128)S(1)} %get-tuple-element.22), channel_id=1, source_target_pairs={{0,2},{1,3},{2,4},{3,5},{4,6},{5,7},{6,8},{7,9},{8,10},{9,11},{10,... | collective-permute-start | bytes 393224 | tf_op jit(solution)/shard_map/ppermute | solution.py:17
  26.5 3.5 %collective-permute-done.2 = f32[4,64,128]{2,1,0:T(8,128)S(1)} collective-permute-done((f32[4,64,128]{2,1,0:T(8,128)S(1)}, f32[4,64,128]{2,1,0:T(8,128)S(1)}, u32[]{:S(2)}, u32[]{:S(2)}) %collective-permute-start.2) | collective-permute-done | bytes 131104 | tf_op jit(solution)/shard_map/ppermute | solution.py:17
  30.1 6.3 %collective-permute-done.3 = f32[4,64,128]{2,1,0:T(8,128)S(1)} collective-permute-done((f32[4,64,128]{2,1,0:T(8,128)S(1)}, f32[4,64,128]{2,1,0:T(8,128)S(1)}, u32[]{:S(2)}, u32[]{:S(2)}) %collective-permute-start.3) | collective-permute-done | bytes 131104 | tf_op jit(solution)/shard_map/ppermute | solution.py:17
  36.4 1.9 %collective-permute-start.4 = (bf16[64,4,128]{2,0,1:T(8,128)(2,1)S(1)}, bf16[64,4,128]{2,0,1:T(8,128)(2,1)S(1)}, u32[]{:S(2)}, u32[]{:S(2)}) collective-permute-start(bf16[64,4,128]{2,0,1:T(8,128)(2,1)S(1)} %copy_bitcast_fusion.3), channel_id=1, source_target_pairs={{0,2},{1,3},{2,4},{3,5},{4,6},{5,7},{6,8},{7,9},{8,10},{9,11},{10,... | collective-permute-start | bytes 196616 | tf_op jit(solution)/shard_map/ppermute | solution.py:17
  38.4 2.5 %collective-permute-start.5 = (bf16[64,4,128]{2,0,1:T(8,128)(2,1)S(1)}, bf16[64,4,128]{2,0,1:T(8,128)(2,1)S(1)}, u32[]{:S(2)}, u32[]{:S(2)}) collective-permute-start(bf16[64,4,128]{2,0,1:T(8,128)(2,1)S(1)} %copy_bitcast_fusion.3), channel_id=1, source_target_pairs={{0,1},{1,2},{2,3},{3,4},{4,5},{5,6},{6,7},{7,8},{8,9},{9,10},{10,1... | collective-permute-start | bytes 196616 | tf_op jit(solution)/shard_map/ppermute | solution.py:17
  40.9 5.5 %collective-permute-start.6 = (bf16[64,4,128]{2,0,1:T(8,128)(2,1)S(1)}, bf16[64,4,128]{2,0,1:T(8,128)(2,1)S(1)}, u32[]{:S(2)}, u32[]{:S(2)}) collective-permute-start(bf16[64,4,128]{2,0,1:T(8,128)(2,1)S(1)} %copy_bitcast_fusion.3), channel_id=1, source_target_pairs={{0,31},{1,0},{2,1},{3,2},{4,3},{5,4},{6,5},{7,6},{8,7},{9,8},{10,9... | collective-permute-start | bytes 196616 | tf_op jit(solution)/shard_map/ppermute | solution.py:17
  46.4 4.8 %collective-permute-start.7 = (bf16[64,4,128]{2,0,1:T(8,128)(2,1)S(1)}, bf16[64,4,128]{2,0,1:T(8,128)(2,1)S(1)}, u32[]{:S(2)}, u32[]{:S(2)}) collective-permute-start(bf16[64,4,128]{2,0,1:T(8,128)(2,1)S(1)} %copy_bitcast_fusion.3), channel_id=1, source_target_pairs={{0,30},{1,31},{2,0},{3,1},{4,2},{5,3},{6,4},{7,5},{8,6},{9,7},{10,... | collective-permute-start | bytes 196616 | tf_op jit(solution)/shard_map/ppermute | solution.py:17
  51.3 2.3 %collective-permute-done.7 = bf16[64,4,128]{2,0,1:T(8,128)(2,1)S(1)} collective-permute-done((bf16[64,4,128]{2,0,1:T(8,128)(2,1)S(1)}, bf16[64,4,128]{2,0,1:T(8,128)(2,1)S(1)}, u32[]{:S(2)}, u32[]{:S(2)}) %collective-permute-start.7) | collective-permute-done | bytes 65568 | tf_op jit(solution)/shard_map/ppermute | solution.py:17
  55.7 2.3 %scatter_fusion.1 = f32[20,64,128]{2,1,0:T(8,128)S(1)} fusion(f32[20,64,128]{2,1,0:T(8,128)S(1)} %broadcast.63.clone, s32[20]{0:T(128)S(1)} %get-tuple-element.8, f32[20,64,128]{2,1,0:T(8,128)S(1)} %convolution_bitcast_fusion.3), kind=kCustom, calls=%fused_computation.5 | custom fusion | flops 163840 | bytes 1966160 | tf_op jit(solution)/shard_map/scatter-add | solution.py:64
  58.0 1.9 %collective-permute-start.10 = (f32[4,64,128]{2,1,0:T(8,128)S(1)}, f32[4,64,128]{2,1,0:T(8,128)S(1)}, u32[]{:S(2)}, u32[]{:S(2)}) collective-permute-start(f32[4,64,128]{2,1,0:T(8,128)S(1)} %get-tuple-element.19), channel_id=1, source_target_pairs={{0,1},{1,2},{2,3},{3,4},{4,5},{5,6},{6,7},{7,8},{8,9},{9,10},{10,1... | collective-permute-start | bytes 393224 | tf_op jit(solution)/shard_map/ppermute | solution.py:17
  59.9 1.9 %collective-permute-start.11 = (f32[4,64,128]{2,1,0:T(8,128)S(1)}, f32[4,64,128]{2,1,0:T(8,128)S(1)}, u32[]{:S(2)}, u32[]{:S(2)}) collective-permute-start(f32[4,64,128]{2,1,0:T(8,128)S(1)} %get-tuple-element.18), channel_id=1, source_target_pairs={{0,2},{1,3},{2,4},{3,5},{4,6},{5,7},{6,8},{7,9},{8,10},{9,11},{10,... | collective-permute-start | bytes 393224 | tf_op jit(solution)/shard_map/ppermute | solution.py:17
  61.9 7.5 %collective-permute-start.8 = (f32[4,64,128]{2,1,0:T(8,128)S(1)}, f32[4,64,128]{2,1,0:T(8,128)S(1)}, u32[]{:S(2)}, u32[]{:S(2)}) collective-permute-start(f32[4,64,128]{2,1,0:T(8,128)S(1)} %get-tuple-element.17), channel_id=1, source_target_pairs={{0,30},{1,31},{2,0},{3,1},{4,2},{5,3},{6,4},{7,5},{8,6},{9,7},{10,... | collective-permute-start | bytes 393224 | tf_op jit(solution)/shard_map/ppermute | solution.py:17
  69.4 3.8 %collective-permute-start.9 = (f32[4,64,128]{2,1,0:T(8,128)S(1)}, f32[4,64,128]{2,1,0:T(8,128)S(1)}, u32[]{:S(2)}, u32[]{:S(2)}) collective-permute-start(f32[4,64,128]{2,1,0:T(8,128)S(1)} %get-tuple-element.20), channel_id=1, source_target_pairs={{0,31},{1,0},{2,1},{3,2},{4,3},{5,4},{6,5},{7,6},{8,7},{9,8},{10,9... | collective-permute-start | bytes 393224 | tf_op jit(solution)/shard_map/ppermute | solution.py:17
  74.1 2.1 %collective-permute-done.9 = f32[4,64,128]{2,1,0:T(8,128)S(1)} collective-permute-done((f32[4,64,128]{2,1,0:T(8,128)S(1)}, f32[4,64,128]{2,1,0:T(8,128)S(1)}, u32[]{:S(2)}, u32[]{:S(2)}) %collective-permute-start.9) | collective-permute-done | bytes 131104 | tf_op jit(solution)/shard_map/ppermute | solution.py:17
  76.4 1.9 %collective-permute-start.12 = (bf16[64,4,128]{2,0,1:T(8,128)(2,1)S(1)}, bf16[64,4,128]{2,0,1:T(8,128)(2,1)S(1)}, u32[]{:S(2)}, u32[]{:S(2)}) collective-permute-start(bf16[64,4,128]{2,0,1:T(8,128)(2,1)S(1)} %bitcast.228), channel_id=1, source_target_pairs={{0,2},{1,3},{2,4},{3,5},{4,6},{5,7},{6,8},{7,9},{8,10},{9,11},{10,... | collective-permute-start | bytes 196616 | tf_op jit(solution)/shard_map/ppermute | solution.py:17
  78.3 2.7 %collective-permute-start.13 = (bf16[64,4,128]{2,0,1:T(8,128)(2,1)S(1)}, bf16[64,4,128]{2,0,1:T(8,128)(2,1)S(1)}, u32[]{:S(2)}, u32[]{:S(2)}) collective-permute-start(bf16[64,4,128]{2,0,1:T(8,128)(2,1)S(1)} %bitcast.229), channel_id=1, source_target_pairs={{0,1},{1,2},{2,3},{3,4},{4,5},{5,6},{6,7},{7,8},{8,9},{9,10},{10,1... | collective-permute-start | bytes 196616 | tf_op jit(solution)/shard_map/ppermute | solution.py:17
  81.0 5.3 %collective-permute-start.14 = (bf16[64,4,128]{2,0,1:T(8,128)(2,1)S(1)}, bf16[64,4,128]{2,0,1:T(8,128)(2,1)S(1)}, u32[]{:S(2)}, u32[]{:S(2)}) collective-permute-start(bf16[64,4,128]{2,0,1:T(8,128)(2,1)S(1)} %bitcast.230), channel_id=1, source_target_pairs={{0,31},{1,0},{2,1},{3,2},{4,3},{5,4},{6,5},{7,6},{8,7},{9,8},{10,9... | collective-permute-start | bytes 196616 | tf_op jit(solution)/shard_map/ppermute | solution.py:17
  86.3 4.8 %collective-permute-start.15 = (bf16[64,4,128]{2,0,1:T(8,128)(2,1)S(1)}, bf16[64,4,128]{2,0,1:T(8,128)(2,1)S(1)}, u32[]{:S(2)}, u32[]{:S(2)}) collective-permute-start(bf16[64,4,128]{2,0,1:T(8,128)(2,1)S(1)} %bitcast.231), channel_id=1, source_target_pairs={{0,30},{1,31},{2,0},{3,1},{4,2},{5,3},{6,4},{7,5},{8,6},{9,7},{10,... | collective-permute-start | bytes 196616 | tf_op jit(solution)/shard_map/ppermute | solution.py:17
  91.2 2.4 %collective-permute-done.15 = bf16[64,4,128]{2,0,1:T(8,128)(2,1)S(1)} collective-permute-done((bf16[64,4,128]{2,0,1:T(8,128)(2,1)S(1)}, bf16[64,4,128]{2,0,1:T(8,128)(2,1)S(1)}, u32[]{:S(2)}, u32[]{:S(2)}) %collective-permute-start.15) | collective-permute-done | bytes 65568 | tf_op jit(solution)/shard_map/ppermute | solution.py:17
  94.9 2.3 %scatter_fusion.2 = f32[20,64,128]{2,1,0:T(8,128)S(1)} fusion(f32[20,64,128]{2,1,0:T(8,128)S(1)} %broadcast.63.clone.2, s32[20]{0:T(128)S(1)} %get-tuple-element.8, f32[20,64,128]{2,1,0:T(8,128)S(1)} %convolution_bitcast_fusion.2), kind=kCustom, calls=%fused_computation.6 | custom fusion | flops 163840 | bytes 1966160 | tf_op jit(solution)/shard_map/scatter-add | solution.py:64
  97.2 7.4 %collective-permute-start.16 = (f32[4,64,128]{2,1,0:T(8,128)S(1)}, f32[4,64,128]{2,1,0:T(8,128)S(1)}, u32[]{:S(2)}, u32[]{:S(2)}) collective-permute-start(f32[4,64,128]{2,1,0:T(8,128)S(1)} %get-tuple-element.13), channel_id=1, source_target_pairs={{0,30},{1,31},{2,0},{3,1},{4,2},{5,3},{6,4},{7,5},{8,6},{9,7},{10,... | collective-permute-start | bytes 393224 | tf_op jit(solution)/shard_map/ppermute | solution.py:17
  104.6 1.9 %collective-permute-start.17 = (f32[4,64,128]{2,1,0:T(8,128)S(1)}, f32[4,64,128]{2,1,0:T(8,128)S(1)}, u32[]{:S(2)}, u32[]{:S(2)}) collective-permute-start(f32[4,64,128]{2,1,0:T(8,128)S(1)} %get-tuple-element.16), channel_id=1, source_target_pairs={{0,31},{1,0},{2,1},{3,2},{4,3},{5,4},{6,5},{7,6},{8,7},{9,8},{10,9... | collective-permute-start | bytes 393224 | tf_op jit(solution)/shard_map/ppermute | solution.py:17
  106.5 3.9 %collective-permute-start.18 = (f32[4,64,128]{2,1,0:T(8,128)S(1)}, f32[4,64,128]{2,1,0:T(8,128)S(1)}, u32[]{:S(2)}, u32[]{:S(2)}) collective-permute-start(f32[4,64,128]{2,1,0:T(8,128)S(1)} %get-tuple-element.15), channel_id=1, source_target_pairs={{0,1},{1,2},{2,3},{3,4},{4,5},{5,6},{6,7},{7,8},{8,9},{9,10},{10,1... | collective-permute-start | bytes 393224 | tf_op jit(solution)/shard_map/ppermute | solution.py:17
  110.5 1.9 %collective-permute-start.19 = (f32[4,64,128]{2,1,0:T(8,128)S(1)}, f32[4,64,128]{2,1,0:T(8,128)S(1)}, u32[]{:S(2)}, u32[]{:S(2)}) collective-permute-start(f32[4,64,128]{2,1,0:T(8,128)S(1)} %get-tuple-element.14), channel_id=1, source_target_pairs={{0,2},{1,3},{2,4},{3,5},{4,6},{5,7},{6,8},{7,9},{8,10},{9,11},{10,... | collective-permute-start | bytes 393224 | tf_op jit(solution)/shard_map/ppermute | solution.py:17
  112.4 3.7 %collective-permute-done.18 = f32[4,64,128]{2,1,0:T(8,128)S(1)} collective-permute-done((f32[4,64,128]{2,1,0:T(8,128)S(1)}, f32[4,64,128]{2,1,0:T(8,128)S(1)}, u32[]{:S(2)}, u32[]{:S(2)}) %collective-permute-start.18) | collective-permute-done | bytes 131104 | tf_op jit(solution)/shard_map/ppermute | solution.py:17
  116.1 6.4 %collective-permute-done.19 = f32[4,64,128]{2,1,0:T(8,128)S(1)} collective-permute-done((f32[4,64,128]{2,1,0:T(8,128)S(1)}, f32[4,64,128]{2,1,0:T(8,128)S(1)}, u32[]{:S(2)}, u32[]{:S(2)}) %collective-permute-start.19) | collective-permute-done | bytes 131104 | tf_op jit(solution)/shard_map/ppermute | solution.py:17
  122.6 1.9 %collective-permute-start.20 = (bf16[64,4,128]{2,0,1:T(8,128)(2,1)S(1)}, bf16[64,4,128]{2,0,1:T(8,128)(2,1)S(1)}, u32[]{:S(2)}, u32[]{:S(2)}) collective-permute-start(bf16[64,4,128]{2,0,1:T(8,128)(2,1)S(1)} %copy_bitcast_fusion.1), channel_id=1, source_target_pairs={{0,2},{1,3},{2,4},{3,5},{4,6},{5,7},{6,8},{7,9},{8,10},{9,11},{10,... | collective-permute-start | bytes 196616 | tf_op jit(solution)/shard_map/ppermute | solution.py:17
  124.5 1.9 %collective-permute-start.21 = (bf16[64,4,128]{2,0,1:T(8,128)(2,1)S(1)}, bf16[64,4,128]{2,0,1:T(8,128)(2,1)S(1)}, u32[]{:S(2)}, u32[]{:S(2)}) collective-permute-start(bf16[64,4,128]{2,0,1:T(8,128)(2,1)S(1)} %copy_bitcast_fusion.1), channel_id=1, source_target_pairs={{0,1},{1,2},{2,3},{3,4},{4,5},{5,6},{6,7},{7,8},{8,9},{9,10},{10,1... | collective-permute-start | bytes 196616 | tf_op jit(solution)/shard_map/ppermute | solution.py:17
  126.4 6.0 %collective-permute-start.22 = (bf16[64,4,128]{2,0,1:T(8,128)(2,1)S(1)}, bf16[64,4,128]{2,0,1:T(8,128)(2,1)S(1)}, u32[]{:S(2)}, u32[]{:S(2)}) collective-permute-start(bf16[64,4,128]{2,0,1:T(8,128)(2,1)S(1)} %copy_bitcast_fusion.1), channel_id=1, source_target_pairs={{0,31},{1,0},{2,1},{3,2},{4,3},{5,4},{6,5},{7,6},{8,7},{9,8},{10,9... | collective-permute-start | bytes 196616 | tf_op jit(solution)/shard_map/ppermute | solution.py:17
  132.5 4.8 %collective-permute-start.23 = (bf16[64,4,128]{2,0,1:T(8,128)(2,1)S(1)}, bf16[64,4,128]{2,0,1:T(8,128)(2,1)S(1)}, u32[]{:S(2)}, u32[]{:S(2)}) collective-permute-start(bf16[64,4,128]{2,0,1:T(8,128)(2,1)S(1)} %copy_bitcast_fusion.1), channel_id=1, source_target_pairs={{0,30},{1,31},{2,0},{3,1},{4,2},{5,3},{6,4},{7,5},{8,6},{9,7},{10,... | collective-permute-start | bytes 196616 | tf_op jit(solution)/shard_map/ppermute | solution.py:17
  137.5 2.3 %collective-permute-done.23 = bf16[64,4,128]{2,0,1:T(8,128)(2,1)S(1)} collective-permute-done((bf16[64,4,128]{2,0,1:T(8,128)(2,1)S(1)}, bf16[64,4,128]{2,0,1:T(8,128)(2,1)S(1)}, u32[]{:S(2)}, u32[]{:S(2)}) %collective-permute-start.23) | collective-permute-done | bytes 65568 | tf_op jit(solution)/shard_map/ppermute | solution.py:17
  141.1 2.3 %scatter_fusion.3 = f32[20,64,128]{2,1,0:T(8,128)S(1)} fusion(f32[20,64,128]{2,1,0:T(8,128)S(1)} %broadcast.63, s32[20]{0:T(128)S(1)} %get-tuple-element.8, f32[20,64,128]{2,1,0:T(8,128)S(1)} %convolution_bitcast_fusion.1), kind=kCustom, calls=%fused_computation.7 | custom fusion | flops 163840 | bytes 1966160 | tf_op jit(solution)/shard_map/scatter-add | solution.py:64
  143.4 7.4 %collective-permute-start.24 = (f32[4,64,128]{2,1,0:T(8,128)S(1)}, f32[4,64,128]{2,1,0:T(8,128)S(1)}, u32[]{:S(2)}, u32[]{:S(2)}) collective-permute-start(f32[4,64,128]{2,1,0:T(8,128)S(1)} %get-tuple-element.9), channel_id=1, source_target_pairs={{0,30},{1,31},{2,0},{3,1},{4,2},{5,3},{6,4},{7,5},{8,6},{9,7},{10,... | collective-permute-start | bytes 393224 | tf_op jit(solution)/shard_map/ppermute | solution.py:17
  150.8 1.9 %collective-permute-start.25 = (f32[4,64,128]{2,1,0:T(8,128)S(1)}, f32[4,64,128]{2,1,0:T(8,128)S(1)}, u32[]{:S(2)}, u32[]{:S(2)}) collective-permute-start(f32[4,64,128]{2,1,0:T(8,128)S(1)} %get-tuple-element.12), channel_id=1, source_target_pairs={{0,31},{1,0},{2,1},{3,2},{4,3},{5,4},{6,5},{7,6},{8,7},{9,8},{10,9... | collective-permute-start | bytes 393224 | tf_op jit(solution)/shard_map/ppermute | solution.py:17
  152.7 3.9 %collective-permute-start.26 = (f32[4,64,128]{2,1,0:T(8,128)S(1)}, f32[4,64,128]{2,1,0:T(8,128)S(1)}, u32[]{:S(2)}, u32[]{:S(2)}) collective-permute-start(f32[4,64,128]{2,1,0:T(8,128)S(1)} %get-tuple-element.11), channel_id=1, source_target_pairs={{0,1},{1,2},{2,3},{3,4},{4,5},{5,6},{6,7},{7,8},{8,9},{9,10},{10,1... | collective-permute-start | bytes 393224 | tf_op jit(solution)/shard_map/ppermute | solution.py:17
  156.7 1.9 %collective-permute-start.27 = (f32[4,64,128]{2,1,0:T(8,128)S(1)}, f32[4,64,128]{2,1,0:T(8,128)S(1)}, u32[]{:S(2)}, u32[]{:S(2)}) collective-permute-start(f32[4,64,128]{2,1,0:T(8,128)S(1)} %get-tuple-element.10), channel_id=1, source_target_pairs={{0,2},{1,3},{2,4},{3,5},{4,6},{5,7},{6,8},{7,9},{8,10},{9,11},{10,... | collective-permute-start | bytes 393224 | tf_op jit(solution)/shard_map/ppermute | solution.py:17
  158.6 3.1 %collective-permute-done.26 = f32[4,64,128]{2,1,0:T(8,128)S(1)} collective-permute-done((f32[4,64,128]{2,1,0:T(8,128)S(1)}, f32[4,64,128]{2,1,0:T(8,128)S(1)}, u32[]{:S(2)}, u32[]{:S(2)}) %collective-permute-start.26) | collective-permute-done | bytes 131104 | tf_op jit(solution)/shard_map/ppermute | solution.py:17
  161.7 6.6 %collective-permute-done.27 = f32[4,64,128]{2,1,0:T(8,128)S(1)} collective-permute-done((f32[4,64,128]{2,1,0:T(8,128)S(1)}, f32[4,64,128]{2,1,0:T(8,128)S(1)}, u32[]{:S(2)}, u32[]{:S(2)}) %collective-permute-start.27) | collective-permute-done | bytes 131104 | tf_op jit(solution)/shard_map/ppermute | solution.py:17
  169.0 1.9 %collective-permute-start.28 = (bf16[64,4,128]{2,0,1:T(8,128)(2,1)S(1)}, bf16[64,4,128]{2,0,1:T(8,128)(2,1)S(1)}, u32[]{:S(2)}, u32[]{:S(2)}) collective-permute-start(bf16[64,4,128]{2,0,1:T(8,128)(2,1)S(1)} %bitcast.232), channel_id=1, source_target_pairs={{0,2},{1,3},{2,4},{3,5},{4,6},{5,7},{6,8},{7,9},{8,10},{9,11},{10,... | collective-permute-start | bytes 196616 | tf_op jit(solution)/shard_map/ppermute | solution.py:17
  171.0 1.9 %collective-permute-start.29 = (bf16[64,4,128]{2,0,1:T(8,128)(2,1)S(1)}, bf16[64,4,128]{2,0,1:T(8,128)(2,1)S(1)}, u32[]{:S(2)}, u32[]{:S(2)}) collective-permute-start(bf16[64,4,128]{2,0,1:T(8,128)(2,1)S(1)} %bitcast.233), channel_id=1, source_target_pairs={{0,1},{1,2},{2,3},{3,4},{4,5},{5,6},{6,7},{7,8},{8,9},{9,10},{10,1... | collective-permute-start | bytes 196616 | tf_op jit(solution)/shard_map/ppermute | solution.py:17
  172.9 6.0 %collective-permute-start.30 = (bf16[64,4,128]{2,0,1:T(8,128)(2,1)S(1)}, bf16[64,4,128]{2,0,1:T(8,128)(2,1)S(1)}, u32[]{:S(2)}, u32[]{:S(2)}) collective-permute-start(bf16[64,4,128]{2,0,1:T(8,128)(2,1)S(1)} %bitcast.234), channel_id=1, source_target_pairs={{0,31},{1,0},{2,1},{3,2},{4,3},{5,4},{6,5},{7,6},{8,7},{9,8},{10,9... | collective-permute-start | bytes 196616 | tf_op jit(solution)/shard_map/ppermute | solution.py:17
  178.9 4.8 %collective-permute-start.31 = (bf16[64,4,128]{2,0,1:T(8,128)(2,1)S(1)}, bf16[64,4,128]{2,0,1:T(8,128)(2,1)S(1)}, u32[]{:S(2)}, u32[]{:S(2)}) collective-permute-start(bf16[64,4,128]{2,0,1:T(8,128)(2,1)S(1)} %bitcast.235), channel_id=1, source_target_pairs={{0,30},{1,31},{2,0},{3,1},{4,2},{5,3},{6,4},{7,5},{8,6},{9,7},{10,... | collective-permute-start | bytes 196616 | tf_op jit(solution)/shard_map/ppermute | solution.py:17
  183.9 2.3 %collective-permute-done.31 = bf16[64,4,128]{2,0,1:T(8,128)(2,1)S(1)} collective-permute-done((bf16[64,4,128]{2,0,1:T(8,128)(2,1)S(1)}, bf16[64,4,128]{2,0,1:T(8,128)(2,1)S(1)}, u32[]{:S(2)}, u32[]{:S(2)}) %collective-permute-start.31) | collective-permute-done | bytes 65568 | tf_op jit(solution)/shard_map/ppermute | solution.py:17
  186.8 1.0 fusion.3
  (86 shorter events, 10.0 us)
Async XLA Ops:
  0.6 1.1 copy-start
  0.6 0.7 copy-start.7
  5.1 21.3 %copy-start.5 = (s32[64,128]{1,0:T(8,128)S(1)}, s32[64,128]{1,0:T(8,128)}, u32[]{:S(2)}) copy-start(s32[64,128]{1,0:T(8,128)} %param.15) | copy-start | bytes 98308
  5.1 31.2 %copy-start.1 = (f32[64,512]{1,0:T(8,128)S(1)}, f32[64,512]{1,0:T(8,128)}, u32[]{:S(2)}) copy-start(f32[64,512]{1,0:T(8,128)} %param.16) | copy-start | bytes 393220
  5.1 31.2 %copy-start.3 = (f32[512]{0:T(512)S(1)}, f32[512]{0:T(512)}, u32[]{:S(2)}) copy-start(f32[512]{0:T(512)} %param.13) | copy-start | bytes 6148
  5.1 31.2 %copy-start.4 = (f32[512]{0:T(512)S(1)}, f32[512]{0:T(512)}, u32[]{:S(2)}) copy-start(f32[512]{0:T(512)} %param.12) | copy-start | bytes 6148
  5.2 21.3 %collective-permute-start = (f32[4,64,128]{2,1,0:T(8,128)S(1)}, f32[4,64,128]{2,1,0:T(8,128)S(1)}, u32[]{:S(2)}, u32[]{:S(2)}) collective-permute-start(f32[4,64,128]{2,1,0:T(8,128)S(1)} %get-tuple-element.21), channel_id=1, source_target_pairs={{0,30},{1,31},{2,0},{3,1},{4,2},{5,3},{6,4},{7,5},{8,6},{9,7},{10,... | collective-permute-start | bytes 393224 | tf_op jit(solution)/shard_map/ppermute | solution.py:17
  18.2 8.4 %collective-permute-start.1 = (f32[4,64,128]{2,1,0:T(8,128)S(1)}, f32[4,64,128]{2,1,0:T(8,128)S(1)}, u32[]{:S(2)}, u32[]{:S(2)}) collective-permute-start(f32[4,64,128]{2,1,0:T(8,128)S(1)} %get-tuple-element.24), channel_id=1, source_target_pairs={{0,31},{1,0},{2,1},{3,2},{4,3},{5,4},{6,5},{7,6},{8,7},{9,8},{10,9... | collective-permute-start | bytes 393224 | tf_op jit(solution)/shard_map/ppermute | solution.py:17
  21.1 9.0 %collective-permute-start.2 = (f32[4,64,128]{2,1,0:T(8,128)S(1)}, f32[4,64,128]{2,1,0:T(8,128)S(1)}, u32[]{:S(2)}, u32[]{:S(2)}) collective-permute-start(f32[4,64,128]{2,1,0:T(8,128)S(1)} %get-tuple-element.23), channel_id=1, source_target_pairs={{0,1},{1,2},{2,3},{3,4},{4,5},{5,6},{6,7},{7,8},{8,9},{9,10},{10,1... | collective-permute-start | bytes 393224 | tf_op jit(solution)/shard_map/ppermute | solution.py:17
  24.0 12.3 %collective-permute-start.3 = (f32[4,64,128]{2,1,0:T(8,128)S(1)}, f32[4,64,128]{2,1,0:T(8,128)S(1)}, u32[]{:S(2)}, u32[]{:S(2)}) collective-permute-start(f32[4,64,128]{2,1,0:T(8,128)S(1)} %get-tuple-element.22), channel_id=1, source_target_pairs={{0,2},{1,3},{2,4},{3,5},{4,6},{5,7},{6,8},{7,9},{8,10},{9,11},{10,... | collective-permute-start | bytes 393224 | tf_op jit(solution)/shard_map/ppermute | solution.py:17
  36.4 14.7 %collective-permute-start.4 = (bf16[64,4,128]{2,0,1:T(8,128)(2,1)S(1)}, bf16[64,4,128]{2,0,1:T(8,128)(2,1)S(1)}, u32[]{:S(2)}, u32[]{:S(2)}) collective-permute-start(bf16[64,4,128]{2,0,1:T(8,128)(2,1)S(1)} %copy_bitcast_fusion.3), channel_id=1, source_target_pairs={{0,2},{1,3},{2,4},{3,5},{4,6},{5,7},{6,8},{7,9},{8,10},{9,11},{10,... | collective-permute-start | bytes 196616 | tf_op jit(solution)/shard_map/ppermute | solution.py:17
  38.4 12.8 %collective-permute-start.5 = (bf16[64,4,128]{2,0,1:T(8,128)(2,1)S(1)}, bf16[64,4,128]{2,0,1:T(8,128)(2,1)S(1)}, u32[]{:S(2)}, u32[]{:S(2)}) collective-permute-start(bf16[64,4,128]{2,0,1:T(8,128)(2,1)S(1)} %copy_bitcast_fusion.3), channel_id=1, source_target_pairs={{0,1},{1,2},{2,3},{3,4},{4,5},{5,6},{6,7},{7,8},{8,9},{9,10},{10,1... | collective-permute-start | bytes 196616 | tf_op jit(solution)/shard_map/ppermute | solution.py:17
  40.9 10.4 %collective-permute-start.6 = (bf16[64,4,128]{2,0,1:T(8,128)(2,1)S(1)}, bf16[64,4,128]{2,0,1:T(8,128)(2,1)S(1)}, u32[]{:S(2)}, u32[]{:S(2)}) collective-permute-start(bf16[64,4,128]{2,0,1:T(8,128)(2,1)S(1)} %copy_bitcast_fusion.3), channel_id=1, source_target_pairs={{0,31},{1,0},{2,1},{3,2},{4,3},{5,4},{6,5},{7,6},{8,7},{9,8},{10,9... | collective-permute-start | bytes 196616 | tf_op jit(solution)/shard_map/ppermute | solution.py:17
  46.4 7.3 %collective-permute-start.7 = (bf16[64,4,128]{2,0,1:T(8,128)(2,1)S(1)}, bf16[64,4,128]{2,0,1:T(8,128)(2,1)S(1)}, u32[]{:S(2)}, u32[]{:S(2)}) collective-permute-start(bf16[64,4,128]{2,0,1:T(8,128)(2,1)S(1)} %copy_bitcast_fusion.3), channel_id=1, source_target_pairs={{0,30},{1,31},{2,0},{3,1},{4,2},{5,3},{6,4},{7,5},{8,6},{9,7},{10,... | collective-permute-start | bytes 196616 | tf_op jit(solution)/shard_map/ppermute | solution.py:17
  53.7 0.8 copy-start.2
  54.3 0.7 copy-start.6
  58.0 15.2 %collective-permute-start.10 = (f32[4,64,128]{2,1,0:T(8,128)S(1)}, f32[4,64,128]{2,1,0:T(8,128)S(1)}, u32[]{:S(2)}, u32[]{:S(2)}) collective-permute-start(f32[4,64,128]{2,1,0:T(8,128)S(1)} %get-tuple-element.19), channel_id=1, source_target_pairs={{0,1},{1,2},{2,3},{3,4},{4,5},{5,6},{6,7},{7,8},{8,9},{9,10},{10,1... | collective-permute-start | bytes 393224 | tf_op jit(solution)/shard_map/ppermute | solution.py:17
  59.9 13.2 %collective-permute-start.11 = (f32[4,64,128]{2,1,0:T(8,128)S(1)}, f32[4,64,128]{2,1,0:T(8,128)S(1)}, u32[]{:S(2)}, u32[]{:S(2)}) collective-permute-start(f32[4,64,128]{2,1,0:T(8,128)S(1)} %get-tuple-element.18), channel_id=1, source_target_pairs={{0,2},{1,3},{2,4},{3,5},{4,6},{5,7},{6,8},{7,9},{8,10},{9,11},{10,... | collective-permute-start | bytes 393224 | tf_op jit(solution)/shard_map/ppermute | solution.py:17
  61.9 12.3 %collective-permute-start.8 = (f32[4,64,128]{2,1,0:T(8,128)S(1)}, f32[4,64,128]{2,1,0:T(8,128)S(1)}, u32[]{:S(2)}, u32[]{:S(2)}) collective-permute-start(f32[4,64,128]{2,1,0:T(8,128)S(1)} %get-tuple-element.17), channel_id=1, source_target_pairs={{0,30},{1,31},{2,0},{3,1},{4,2},{5,3},{6,4},{7,5},{8,6},{9,7},{10,... | collective-permute-start | bytes 393224 | tf_op jit(solution)/shard_map/ppermute | solution.py:17
  69.4 6.9 %collective-permute-start.9 = (f32[4,64,128]{2,1,0:T(8,128)S(1)}, f32[4,64,128]{2,1,0:T(8,128)S(1)}, u32[]{:S(2)}, u32[]{:S(2)}) collective-permute-start(f32[4,64,128]{2,1,0:T(8,128)S(1)} %get-tuple-element.20), channel_id=1, source_target_pairs={{0,31},{1,0},{2,1},{3,2},{4,3},{5,4},{6,5},{7,6},{8,7},{9,8},{10,9... | collective-permute-start | bytes 393224 | tf_op jit(solution)/shard_map/ppermute | solution.py:17
  76.4 14.7 %collective-permute-start.12 = (bf16[64,4,128]{2,0,1:T(8,128)(2,1)S(1)}, bf16[64,4,128]{2,0,1:T(8,128)(2,1)S(1)}, u32[]{:S(2)}, u32[]{:S(2)}) collective-permute-start(bf16[64,4,128]{2,0,1:T(8,128)(2,1)S(1)} %bitcast.228), channel_id=1, source_target_pairs={{0,2},{1,3},{2,4},{3,5},{4,6},{5,7},{6,8},{7,9},{8,10},{9,11},{10,... | collective-permute-start | bytes 196616 | tf_op jit(solution)/shard_map/ppermute | solution.py:17
  78.3 12.8 %collective-permute-start.13 = (bf16[64,4,128]{2,0,1:T(8,128)(2,1)S(1)}, bf16[64,4,128]{2,0,1:T(8,128)(2,1)S(1)}, u32[]{:S(2)}, u32[]{:S(2)}) collective-permute-start(bf16[64,4,128]{2,0,1:T(8,128)(2,1)S(1)} %bitcast.229), channel_id=1, source_target_pairs={{0,1},{1,2},{2,3},{3,4},{4,5},{5,6},{6,7},{7,8},{8,9},{9,10},{10,1... | collective-permute-start | bytes 196616 | tf_op jit(solution)/shard_map/ppermute | solution.py:17
  81.0 10.2 %collective-permute-start.14 = (bf16[64,4,128]{2,0,1:T(8,128)(2,1)S(1)}, bf16[64,4,128]{2,0,1:T(8,128)(2,1)S(1)}, u32[]{:S(2)}, u32[]{:S(2)}) collective-permute-start(bf16[64,4,128]{2,0,1:T(8,128)(2,1)S(1)} %bitcast.230), channel_id=1, source_target_pairs={{0,31},{1,0},{2,1},{3,2},{4,3},{5,4},{6,5},{7,6},{8,7},{9,8},{10,9... | collective-permute-start | bytes 196616 | tf_op jit(solution)/shard_map/ppermute | solution.py:17
  86.3 7.3 %collective-permute-start.15 = (bf16[64,4,128]{2,0,1:T(8,128)(2,1)S(1)}, bf16[64,4,128]{2,0,1:T(8,128)(2,1)S(1)}, u32[]{:S(2)}, u32[]{:S(2)}) collective-permute-start(bf16[64,4,128]{2,0,1:T(8,128)(2,1)S(1)} %bitcast.231), channel_id=1, source_target_pairs={{0,30},{1,31},{2,0},{3,1},{4,2},{5,3},{6,4},{7,5},{8,6},{9,7},{10,... | collective-permute-start | bytes 196616 | tf_op jit(solution)/shard_map/ppermute | solution.py:17
  97.2 15.2 %collective-permute-start.16 = (f32[4,64,128]{2,1,0:T(8,128)S(1)}, f32[4,64,128]{2,1,0:T(8,128)S(1)}, u32[]{:S(2)}, u32[]{:S(2)}) collective-permute-start(f32[4,64,128]{2,1,0:T(8,128)S(1)} %get-tuple-element.13), channel_id=1, source_target_pairs={{0,30},{1,31},{2,0},{3,1},{4,2},{5,3},{6,4},{7,5},{8,6},{9,7},{10,... | collective-permute-start | bytes 393224 | tf_op jit(solution)/shard_map/ppermute | solution.py:17
  104.6 7.8 %collective-permute-start.17 = (f32[4,64,128]{2,1,0:T(8,128)S(1)}, f32[4,64,128]{2,1,0:T(8,128)S(1)}, u32[]{:S(2)}, u32[]{:S(2)}) collective-permute-start(f32[4,64,128]{2,1,0:T(8,128)S(1)} %get-tuple-element.16), channel_id=1, source_target_pairs={{0,31},{1,0},{2,1},{3,2},{4,3},{5,4},{6,5},{7,6},{8,7},{9,8},{10,9... | collective-permute-start | bytes 393224 | tf_op jit(solution)/shard_map/ppermute | solution.py:17
  106.5 9.5 %collective-permute-start.18 = (f32[4,64,128]{2,1,0:T(8,128)S(1)}, f32[4,64,128]{2,1,0:T(8,128)S(1)}, u32[]{:S(2)}, u32[]{:S(2)}) collective-permute-start(f32[4,64,128]{2,1,0:T(8,128)S(1)} %get-tuple-element.15), channel_id=1, source_target_pairs={{0,1},{1,2},{2,3},{3,4},{4,5},{5,6},{6,7},{7,8},{8,9},{9,10},{10,1... | collective-permute-start | bytes 393224 | tf_op jit(solution)/shard_map/ppermute | solution.py:17
  110.5 12.0 %collective-permute-start.19 = (f32[4,64,128]{2,1,0:T(8,128)S(1)}, f32[4,64,128]{2,1,0:T(8,128)S(1)}, u32[]{:S(2)}, u32[]{:S(2)}) collective-permute-start(f32[4,64,128]{2,1,0:T(8,128)S(1)} %get-tuple-element.14), channel_id=1, source_target_pairs={{0,2},{1,3},{2,4},{3,5},{4,6},{5,7},{6,8},{7,9},{8,10},{9,11},{10,... | collective-permute-start | bytes 393224 | tf_op jit(solution)/shard_map/ppermute | solution.py:17
  122.6 14.7 %collective-permute-start.20 = (bf16[64,4,128]{2,0,1:T(8,128)(2,1)S(1)}, bf16[64,4,128]{2,0,1:T(8,128)(2,1)S(1)}, u32[]{:S(2)}, u32[]{:S(2)}) collective-permute-start(bf16[64,4,128]{2,0,1:T(8,128)(2,1)S(1)} %copy_bitcast_fusion.1), channel_id=1, source_target_pairs={{0,2},{1,3},{2,4},{3,5},{4,6},{5,7},{6,8},{7,9},{8,10},{9,11},{10,... | collective-permute-start | bytes 196616 | tf_op jit(solution)/shard_map/ppermute | solution.py:17
  124.5 12.8 %collective-permute-start.21 = (bf16[64,4,128]{2,0,1:T(8,128)(2,1)S(1)}, bf16[64,4,128]{2,0,1:T(8,128)(2,1)S(1)}, u32[]{:S(2)}, u32[]{:S(2)}) collective-permute-start(bf16[64,4,128]{2,0,1:T(8,128)(2,1)S(1)} %copy_bitcast_fusion.1), channel_id=1, source_target_pairs={{0,1},{1,2},{2,3},{3,4},{4,5},{5,6},{6,7},{7,8},{8,9},{9,10},{10,1... | collective-permute-start | bytes 196616 | tf_op jit(solution)/shard_map/ppermute | solution.py:17
  126.4 11.0 %collective-permute-start.22 = (bf16[64,4,128]{2,0,1:T(8,128)(2,1)S(1)}, bf16[64,4,128]{2,0,1:T(8,128)(2,1)S(1)}, u32[]{:S(2)}, u32[]{:S(2)}) collective-permute-start(bf16[64,4,128]{2,0,1:T(8,128)(2,1)S(1)} %copy_bitcast_fusion.1), channel_id=1, source_target_pairs={{0,31},{1,0},{2,1},{3,2},{4,3},{5,4},{6,5},{7,6},{8,7},{9,8},{10,9... | collective-permute-start | bytes 196616 | tf_op jit(solution)/shard_map/ppermute | solution.py:17
  132.5 7.3 %collective-permute-start.23 = (bf16[64,4,128]{2,0,1:T(8,128)(2,1)S(1)}, bf16[64,4,128]{2,0,1:T(8,128)(2,1)S(1)}, u32[]{:S(2)}, u32[]{:S(2)}) collective-permute-start(bf16[64,4,128]{2,0,1:T(8,128)(2,1)S(1)} %copy_bitcast_fusion.1), channel_id=1, source_target_pairs={{0,30},{1,31},{2,0},{3,1},{4,2},{5,3},{6,4},{7,5},{8,6},{9,7},{10,... | collective-permute-start | bytes 196616 | tf_op jit(solution)/shard_map/ppermute | solution.py:17
  143.4 15.2 %collective-permute-start.24 = (f32[4,64,128]{2,1,0:T(8,128)S(1)}, f32[4,64,128]{2,1,0:T(8,128)S(1)}, u32[]{:S(2)}, u32[]{:S(2)}) collective-permute-start(f32[4,64,128]{2,1,0:T(8,128)S(1)} %get-tuple-element.9), channel_id=1, source_target_pairs={{0,30},{1,31},{2,0},{3,1},{4,2},{5,3},{6,4},{7,5},{8,6},{9,7},{10,... | collective-permute-start | bytes 393224 | tf_op jit(solution)/shard_map/ppermute | solution.py:17
  150.8 7.8 %collective-permute-start.25 = (f32[4,64,128]{2,1,0:T(8,128)S(1)}, f32[4,64,128]{2,1,0:T(8,128)S(1)}, u32[]{:S(2)}, u32[]{:S(2)}) collective-permute-start(f32[4,64,128]{2,1,0:T(8,128)S(1)} %get-tuple-element.12), channel_id=1, source_target_pairs={{0,31},{1,0},{2,1},{3,2},{4,3},{5,4},{6,5},{7,6},{8,7},{9,8},{10,9... | collective-permute-start | bytes 393224 | tf_op jit(solution)/shard_map/ppermute | solution.py:17
  152.7 9.0 %collective-permute-start.26 = (f32[4,64,128]{2,1,0:T(8,128)S(1)}, f32[4,64,128]{2,1,0:T(8,128)S(1)}, u32[]{:S(2)}, u32[]{:S(2)}) collective-permute-start(f32[4,64,128]{2,1,0:T(8,128)S(1)} %get-tuple-element.11), channel_id=1, source_target_pairs={{0,1},{1,2},{2,3},{3,4},{4,5},{5,6},{6,7},{7,8},{8,9},{9,10},{10,1... | collective-permute-start | bytes 393224 | tf_op jit(solution)/shard_map/ppermute | solution.py:17
  156.7 11.6 %collective-permute-start.27 = (f32[4,64,128]{2,1,0:T(8,128)S(1)}, f32[4,64,128]{2,1,0:T(8,128)S(1)}, u32[]{:S(2)}, u32[]{:S(2)}) collective-permute-start(f32[4,64,128]{2,1,0:T(8,128)S(1)} %get-tuple-element.10), channel_id=1, source_target_pairs={{0,2},{1,3},{2,4},{3,5},{4,6},{5,7},{6,8},{7,9},{8,10},{9,11},{10,... | collective-permute-start | bytes 393224 | tf_op jit(solution)/shard_map/ppermute | solution.py:17
  169.0 14.7 %collective-permute-start.28 = (bf16[64,4,128]{2,0,1:T(8,128)(2,1)S(1)}, bf16[64,4,128]{2,0,1:T(8,128)(2,1)S(1)}, u32[]{:S(2)}, u32[]{:S(2)}) collective-permute-start(bf16[64,4,128]{2,0,1:T(8,128)(2,1)S(1)} %bitcast.232), channel_id=1, source_target_pairs={{0,2},{1,3},{2,4},{3,5},{4,6},{5,7},{6,8},{7,9},{8,10},{9,11},{10,... | collective-permute-start | bytes 196616 | tf_op jit(solution)/shard_map/ppermute | solution.py:17
  171.0 12.8 %collective-permute-start.29 = (bf16[64,4,128]{2,0,1:T(8,128)(2,1)S(1)}, bf16[64,4,128]{2,0,1:T(8,128)(2,1)S(1)}, u32[]{:S(2)}, u32[]{:S(2)}) collective-permute-start(bf16[64,4,128]{2,0,1:T(8,128)(2,1)S(1)} %bitcast.233), channel_id=1, source_target_pairs={{0,1},{1,2},{2,3},{3,4},{4,5},{5,6},{6,7},{7,8},{8,9},{9,10},{10,1... | collective-permute-start | bytes 196616 | tf_op jit(solution)/shard_map/ppermute | solution.py:17
  172.9 11.0 %collective-permute-start.30 = (bf16[64,4,128]{2,0,1:T(8,128)(2,1)S(1)}, bf16[64,4,128]{2,0,1:T(8,128)(2,1)S(1)}, u32[]{:S(2)}, u32[]{:S(2)}) collective-permute-start(bf16[64,4,128]{2,0,1:T(8,128)(2,1)S(1)} %bitcast.234), channel_id=1, source_target_pairs={{0,31},{1,0},{2,1},{3,2},{4,3},{5,4},{6,5},{7,6},{8,7},{9,8},{10,9... | collective-permute-start | bytes 196616 | tf_op jit(solution)/shard_map/ppermute | solution.py:17
  178.9 7.3 %collective-permute-start.31 = (bf16[64,4,128]{2,0,1:T(8,128)(2,1)S(1)}, bf16[64,4,128]{2,0,1:T(8,128)(2,1)S(1)}, u32[]{:S(2)}, u32[]{:S(2)}) collective-permute-start(bf16[64,4,128]{2,0,1:T(8,128)(2,1)S(1)} %bitcast.235), channel_id=1, source_target_pairs={{0,30},{1,31},{2,0},{3,1},{4,2},{5,3},{6,4},{7,5},{8,6},{9,7},{10,... | collective-permute-start | bytes 196616 | tf_op jit(solution)/shard_map/ppermute | solution.py:17
where the time goes:
time: 189 us; the launch traced here: 188 us
  starting transfers between devices  125 us (66%)
  waiting for transfers between devices  42 us (22%)
  other arithmetic  10.3 us (5%)
  local copies, waits for them, and re-layouts  4.84 us (3%)
  matrix products  3.89 us (2%)
    ppermute x32, starting transfers between devices, shifted(): return lax.ppermute(value, axis, pairs)  125 us
    ppermute x32, waiting for transfers between devices, shifted(): return lax.ppermute(value, axis, pairs)  42 us
    scatter-add x4, other arithmetic, per_device(): spread = jax.ops.segment_sum(partial_terms, local, num_segments=spans)  9.08 us
  transfers between devices with their start and end apart: 32, of which 13 were waited for; matrix products, arithmetic and copies ran while one was open for 0% of the time, Pallas kernels for 0%

commit v1 on v0

v1 whole, which is shorter than its diff:
```python
import functools

import jax
import jax.numpy as jnp
from jax import lax
from jax.experimental import pallas as pl
from jax.experimental.pallas import tpu as pltpu
from jax.sharding import PartitionSpec as P

MESH = pl.DeviceIdType.MESH

REACH = 2
ITERS = 4
SPAN = 2 * REACH + 1
OFFSETS = (-2, 2, -1, 1)

step_primal = 0.4
step_dual = 0.4


def kernel(
    n_dev,
    idx_ref,
    blocks_ref,
    cost_ref,
    upper_ref,
    cap_ref,
    dis_ref,
    xs_ref,
    ys_ref,
    x_out,
    y_out,
    kb,
    head,
    head_in,
    ysend,
    yin,
    zsend,
    zin,
    zown,
    x,
    y,
    cost,
    upper,
    cap,
    dis,
    bound,
    load_sem,
    kb_send,
    kb_recv,
    y_sends,
    y_recvs,
    z_sends,
    z_recvs,
):
    per = kb.shape[1]
    width = kb.shape[2]
    scen = x.shape[0]
    me = lax.axis_index("blk")

    def remote(source, target, send, recv, offset):
        return pltpu.make_async_remote_copy(
            src_ref=source,
            dst_ref=target,
            send_sem=send,
            recv_sem=recv,
            device_id={"blk": lax.rem(me + offset + n_dev, n_dev)},
            device_id_type=MESH,
        )

    loads = [
        pltpu.make_async_copy(ys_ref, y, load_sem.at[0]),
        pltpu.make_async_copy(blocks_ref.at[0, pl.ds(REACH * per, per)], kb.at[REACH], load_sem.at[1]),
        pltpu.make_async_copy(xs_ref, x, load_sem.at[2]),
        pltpu.make_async_copy(cost_ref, cost, load_sem.at[3]),
        pltpu.make_async_copy(upper_ref, upper, load_sem.at[4]),
        pltpu.make_async_copy(cap_ref, cap, load_sem.at[5]),
        pltpu.make_async_copy(dis_ref, dis, load_sem.at[6]),
    ]
    for load in loads:
        load.start()

    barrier = pltpu.get_barrier_semaphore()
    for offset in OFFSETS:
        pl.semaphore_signal(
            barrier, inc=1, device_id={"blk": lax.rem(me + offset + n_dev, n_dev)}, device_id_type=MESH
        )

    head[pl.ds(scen, head.shape[0] - scen), :] = jnp.zeros((head.shape[0] - scen, width), jnp.float32)
    for slot in range(SPAN * per):
        head[pl.ds(scen + slot, 1), :] = jnp.full((1, width), lax.rem(idx_ref[0, slot], per), jnp.float32)
    loads[0].wait()
    head[pl.ds(0, scen), :] = y[...].astype(jnp.bfloat16).astype(jnp.float32)
    ysend[0] = head[...].astype(jnp.bfloat16)

    pl.semaphore_wait(barrier, 2 * REACH)

    heads = {o: remote(ysend.at[0], head_in.at[REACH - o], y_sends.at[0, REACH - o], y_recvs.at[0, REACH - o], o) for o in OFFSETS}
    for o in OFFSETS:
        heads[o].start()
    blocks_out = {
        o: remote(
            blocks_ref.at[0, pl.ds((REACH + o) * per, per)],
            kb.at[REACH - o],
            kb_send.at[REACH - o],
            kb_recv.at[REACH - o],
            o,
        )
        for o in OFFSETS
    }
    for o in (-1, 1, -2, 2):
        blocks_out[o].start()

    for load in loads[1:]:
        load.wait()
    bound[...] = cap[...] * jnp.where(dis[...] == 1, 0.25, 1.0)

    def blocks_of(j):
        return jnp.concatenate([kb[j, s] for s in range(per)], axis=1)

    def marks(j):
        base = scen + (SPAN - 1 - j) * per
        source = head if j == REACH else head_in.at[j]
        rows = source[pl.ds(base, per), :].astype(jnp.float32)
        return [jnp.broadcast_to(rows[s : s + 1, :], (scen, width)) for s in range(per)]

    for it in range(ITERS):
        last = it == ITERS - 1
        acc = [jnp.broadcast_to(cost[:, pl.ds(c * width, width)], (scen, width)) for c in range(per)]
        for j in (2, 1, 3, 0, 4):
            if j == REACH:
                low = ysend[it, pl.ds(0, scen), :]
            else:
                if it == 0:
                    heads[REACH - j].wait_recv()
                    blocks_out[REACH - j].wait_recv()
                    low = head_in[j, pl.ds(0, scen), :]
                else:
                    remote(ysend.at[it, pl.ds(0, scen)], yin.at[it - 1, j], y_sends.at[it, j], y_recvs.at[it, j], REACH - j).wait_recv()
                    low = yin[it - 1, j]
            terms = jnp.dot(low, blocks_of(j), preferred_element_type=jnp.float32)
            acc[0] = acc[0] + terms[:, :width]
            acc[per - 1] = acc[per - 1] + terms[:, width : 2 * width]
            mark = marks(j)
            for s in range(2, per):
                part = terms[:, s * width : (s + 1) * width]
                for c in range(per):
                    acc[c] = acc[c] + jnp.where(mark[s] == c, part, 0.0)
        bars = []
        for c in range(per):
            cols = pl.ds(c * width, width)
            old = x[:, cols]
            new = jnp.minimum(jnp.maximum(old - step_primal * acc[c], 0.0), upper[:, cols])
            bars.append((2.0 * new - old).astype(jnp.bfloat16))
            x[:, cols] = new
        if last:
            x_store = pltpu.make_async_copy(x, x_out, load_sem.at[0])
            x_store.start()
        for j in (0, 4, 1, 3, 2):
            mark = marks(j)
            picked = [bars[0], bars[per - 1]]
            for s in range(2, per):
                chosen = bars[0].astype(jnp.float32)
                for c in range(1, per):
                    chosen = jnp.where(mark[s] == c, bars[c].astype(jnp.float32), chosen)
                picked.append(chosen.astype(jnp.bfloat16))
            terms = lax.dot_general(
                jnp.concatenate(picked, axis=1),
                blocks_of(j),
                (((1,), (1,)), ((), ())),
                preferred_element_type=jnp.float32,
            )
            if j == REACH:
                zown[...] = terms
            else:
                zsend[it, j] = terms
                remote(zsend.at[it, j], zin.at[it, 2 * REACH - j], z_sends.at[it, j], z_recvs.at[it, 2 * REACH - j], j - REACH).start()
        total = zown[...]
        for j in (1, 3, 0, 4):
            remote(zsend.at[it, j], zin.at[it, j], z_sends.at[it, j], z_recvs.at[it, j], REACH - j).wait_recv()
            total = total + zin[it, j]
        new_y = jnp.maximum(y[...] + step_dual * (total - bound[...]), 0.0)
        y[...] = new_y
        if not last:
            ysend[it + 1, pl.ds(0, scen), :] = new_y.astype(jnp.bfloat16)
            for o in OFFSETS:
                remote(
                    ysend.at[it + 1, pl.ds(0, scen)],
                    yin.at[it, REACH - o],
                    y_sends.at[it + 1, REACH - o],
                    y_recvs.at[it + 1, REACH - o],
                    o,
                ).start()
    y_store = pltpu.make_async_copy(y, y_out, load_sem.at[1])
    y_store.start()
    for o in OFFSETS:
        heads[o].wait_send()
        blocks_out[o].wait_send()
        for it in range(1, ITERS):
            remote(ysend.at[it, pl.ds(0, scen)], yin.at[it - 1, REACH - o], y_sends.at[it, REACH - o], y_recvs.at[it, REACH - o], o).wait_send()
        for it in range(ITERS):
            j = o + REACH
            remote(zsend.at[it, j], zin.at[it, j], z_sends.at[it, j], z_recvs.at[it, j], o).wait_send()
    x_store.wait()
    y_store.wait()


def per_device(n_dev, blocks, col_index, cost, upper, capacity, disrupted, x_start, y_start):
    slots, width = blocks.shape[1], blocks.shape[3]
    per = slots // SPAN
    scen, ncols = x_start.shape
    rows_head = scen + 32
    f32, bf16 = jnp.float32, jnp.bfloat16
    anyspace = pl.BlockSpec(memory_space=pl.ANY)
    dma = pltpu.SemaphoreType.DMA
    return pl.pallas_call(
        functools.partial(kernel, n_dev),
        out_shape=(
            jax.ShapeDtypeStruct(x_start.shape, f32),
            jax.ShapeDtypeStruct(y_start.shape, f32),
        ),
        in_specs=[pl.BlockSpec(memory_space=pltpu.SMEM)] + [anyspace] * 7,
        out_specs=(anyspace, anyspace),
        scratch_shapes=[
            pltpu.VMEM((SPAN, per, width, width), bf16),
            pltpu.VMEM((rows_head, width), f32),
            pltpu.VMEM((SPAN, rows_head, width), bf16),
            pltpu.VMEM((ITERS, rows_head, width), bf16),
            pltpu.VMEM((ITERS - 1, SPAN, scen, width), bf16),
            pltpu.VMEM((ITERS, SPAN, scen, width), f32),
            pltpu.VMEM((ITERS, SPAN, scen, width), f32),
            pltpu.VMEM((scen, width), f32),
            pltpu.VMEM((scen, ncols), f32),
            pltpu.VMEM((scen, width), f32),
            pltpu.VMEM((1, ncols), f32),
            pltpu.VMEM((1, ncols), f32),
            pltpu.VMEM((1, width), f32),
            pltpu.VMEM((scen, width), jnp.int32),
            pltpu.VMEM((scen, width), f32),
            dma((7,)),
            dma((SPAN,)),
            dma((SPAN,)),
            dma((ITERS, SPAN)),
            dma((ITERS, SPAN)),
            dma((ITERS, SPAN)),
            dma((ITERS, SPAN)),
        ],
        compiler_params=pltpu.CompilerParams(
            collective_id=0, has_side_effects=True, vmem_limit_bytes=32 * 1024 * 1024
        ),
    )(
        col_index,
        blocks,
        cost.reshape(1, -1),
        upper.reshape(1, -1),
        capacity.reshape(1, -1),
        disrupted,
        x_start,
        y_start,
    )


def solution(mesh):
    placed = (
        P(("scen", "blk"), None, None, None),
        P(("scen", "blk"), None),
        P(("scen", "blk")),
        P(("scen", "blk")),
        P(("scen", "blk")),
        P("scen", "blk"),
        P("scen", "blk"),
        P("scen", "blk"),
    )
    return jax.shard_map(
        functools.partial(per_device, mesh.shape["blk"]),
        mesh=mesh,
        in_specs=placed,
        out_specs=(P("scen", "blk"), P("scen", "blk")),
        check_vma=False,
    )
```

time: 189 us -> 67.4 us (0.36)
  starting transfers between devices: 125 us -> 0 us
  Pallas kernels: 0 us -> 60.9 us
  waiting for transfers between devices: 42 us -> 0 us
  other arithmetic: 10.3 us -> 0 us
  matrix products: 3.89 us -> 0 us
    ppermute x32 -> x0, starting transfers between devices: 125 us -> none  [shifted(): return lax.ppermute(value, axis, pairs)]
    pallas_call x0 -> x1, Pallas kernels: none -> 60.9 us  [per_device(): pl.pallas_call(functools.partial(kernel, n_dev), out_shape=(jax.ShapeDtyp...]
    ppermute x32 -> x0, waiting for transfers between devices: 42 us -> none  [shifted(): return lax.ppermute(value, axis, pairs)]
    scatter-add x4 -> x0, other arithmetic: 9.08 us -> none  [per_device(): spread = jax.ops.segment_sum(partial_terms, local, num_segments=spans)]
    dot_general x8 -> x0, matrix products: 3.89 us -> none  [the longest x4 2.17 us: per_device(): jnp.einsum('ufol,foql->ufq', selected_entries, blocks, preferred_element_...]
    unnamed x30 -> x18, local copies, waits for them, and re-layouts: 1.93 us -> 5.45 us
    gather x4 -> x0, local copies, waits for them, and re-layouts: 2.44 us -> none  [per_device(): jnp.take(window, local, axis=1).reshape(scen, rows_here, slots, width)]
  transfers between devices with their start and end apart: 32 -> 0, of which waited for: 13 -> 0; matrix products, arithmetic and copies ran while one was open for 0% -> 0% of each run, Pallas kernels for 0% -> 0%
where the time goes in v1:
time: 67.4 us; the launch traced here: 67 us
  Pallas kernels  60.9 us (90%)
  local copies, waits for them, and re-layouts  5.45 us (8%)
  between operations  0.68 us (1%)
    pallas_call x1, Pallas kernels, per_device(): pl.pallas_call(functools.partial(kernel, n_dev), out_shape=(jax.ShapeDtyp...  60.9 us
    unnamed x18, local copies, waits for them, and re-layouts  5.45 us

profile of v1, /device:TPU:6, one launch (start us, length us, event | category | flops | bytes accessed | tf_op | source)
XLA Modules:
  0.0 67.0 jit_solution(14043961998355337662)
XLA Ops:
  0.6 0.0 copy-start.5
  0.6 0.0 copy-start.4
  0.7 0.0 copy-start.6
  0.7 0.0 copy-start.7
  0.7 0.6 copy-done.5
  1.3 0.0 copy-done.4
  1.3 0.0 copy-done.6
  1.3 0.0 copy-done.7
  1.3 0.0 copy-start
  1.3 1.1 %copy-done = bf16[1,20,128,128]{3,2,1,0:T(8,128)(2,1)S(1)} copy-done((bf16[1,20,128,128]{3,2,1,0:T(8,128)(2,1)S(1)}, bf16[1,20,128,128]{3,2,1,0:T(8,128)(2,1)}, u32[]{:S(2)}) %copy-start) | copy-done | bytes 655384
  2.4 0.0 copy-start.1
  2.4 0.9 %copy-done.1 = f32[64,512]{1,0:T(8,128)S(1)} copy-done((f32[64,512]{1,0:T(8,128)S(1)}, f32[64,512]{1,0:T(8,128)}, u32[]{:S(2)}) %copy-start.1) | copy-done | bytes 131096
  3.3 0.0 copy-start.2
  3.3 0.8 %copy-done.2 = s32[64,128]{1,0:T(8,128)S(1)} copy-done((s32[64,128]{1,0:T(8,128)S(1)}, s32[64,128]{1,0:T(8,128)}, u32[]{:S(2)}) %copy-start.2) | copy-done | bytes 32792
  4.1 0.0 copy-start.3
  4.1 0.8 %copy-done.3 = f32[64,128]{1,0:T(8,128)S(1)} copy-done((f32[64,128]{1,0:T(8,128)S(1)}, f32[64,128]{1,0:T(8,128)}, u32[]{:S(2)}) %copy-start.3) | copy-done | bytes 32792
  4.8 60.9 %shard_map.95 = (f32[64,512]{1,0:T(8,128)S(1)}, f32[64,128]{1,0:T(8,128)S(1)}) custom-call(s32[1,20]{1,0:T(1,128)S(1)} %copy-done.6, bf16[1,20,128,128]{3,2,1,0:T(8,128)(2,1)S(1)} %copy-done, f32[1,512]{1,0:T(1,128)S(1)} %bitcast.3, f32[1,512]{1,0:T(1,128)S(1)} %bitcast.4, f32[1,128]{1,0:T(1,128)S(1)} %bitcast.5, s32[64,128]{1,0:T(8,128)S(1)} %copy-done.2, ...), custom_call_target="tpu_custom_call" | custom-call | tf_op jit(solution)/shard_map/pallas_call | solution.py:216
  65.8 0.7 copy.12
  66.4 0.6 copy.13
Async XLA Ops:
  0.6 0.7 %copy-start.5 = (f32[512]{0:T(512)S(1)}, f32[512]{0:T(512)}, u32[]{:S(2)}) copy-start(f32[512]{0:T(512)} %param.11) | copy-start | bytes 6148
  0.6 0.7 %copy-start.4 = (f32[512]{0:T(512)S(1)}, f32[512]{0:T(512)}, u32[]{:S(2)}) copy-start(f32[512]{0:T(512)} %param.10) | copy-start | bytes 6148
  0.7 0.7 %copy-start.6 = (s32[1,20]{1,0:T(1,128)S(1)}, s32[1,20]{1,0:T(1,128)}, u32[]{:S(2)}) copy-start(s32[1,20]{1,0:T(1,128)} %idx_ref.1) | copy-start | bytes 244
  0.7 0.7 %copy-start.7 = (f32[128]{0:T(128)S(1)}, f32[128]{0:T(128)}, u32[]{:S(2)}) copy-start(f32[128]{0:T(128)} %param.12) | copy-start | bytes 1540
  1.3 1.1 %copy-start = (bf16[1,20,128,128]{3,2,1,0:T(8,128)(2,1)S(1)}, bf16[1,20,128,128]{3,2,1,0:T(8,128)(2,1)}, u32[]{:S(2)}) copy-start(bf16[1,20,128,128]{3,2,1,0:T(8,128)(2,1)} %blocks_ref.1) | copy-start | bytes 1966084
  2.4 0.9 %copy-start.1 = (f32[64,512]{1,0:T(8,128)S(1)}, f32[64,512]{1,0:T(8,128)}, u32[]{:S(2)}) copy-start(f32[64,512]{1,0:T(8,128)} %xs_ref.1) | copy-start | bytes 393220
  3.3 0.8 %copy-start.2 = (s32[64,128]{1,0:T(8,128)S(1)}, s32[64,128]{1,0:T(8,128)}, u32[]{:S(2)}) copy-start(s32[64,128]{1,0:T(8,128)} %dis_ref.1) | copy-start | bytes 98308
  4.1 0.8 %copy-start.3 = (f32[64,128]{1,0:T(8,128)S(1)}, f32[64,128]{1,0:T(8,128)}, u32[]{:S(2)}) copy-start(f32[64,128]{1,0:T(8,128)} %ys_ref.1) | copy-start | bytes 98308

commit v2 on v1

--- a/solution.py
+++ b/solution.py
@@ -20,7 +20,8 @@
 
 def kernel(
     n_dev,
-    idx_ref,
+    paired,
+    idx_hbm,
     blocks_ref,
     cost_ref,
     upper_ref,
@@ -30,6 +31,7 @@
     ys_ref,
     x_out,
     y_out,
+    idx_ref,
     kb,
     head,
     head_in,
@@ -38,6 +40,8 @@
     zsend,
     zin,
     zown,
+    zheld,
+    zsum,
     x,
     y,
     cost,
@@ -52,6 +56,7 @@
     y_recvs,
     z_sends,
     z_recvs,
+    turn,
 ):
     per = kb.shape[1]
     width = kb.shape[2]
@@ -68,8 +73,20 @@
             device_id_type=MESH,
         )
 
+    barrier = pltpu.get_barrier_semaphore()
+    for offset in OFFSETS:
+        pl.semaphore_signal(
+            barrier, inc=1, device_id={"blk": lax.rem(me + offset + n_dev, n_dev)}, device_id_type=MESH
+        )
+    if paired:
+        group = lax.axis_index("scen")
+        second = lax.rem(group, 2)
+        twin = {"scen": group + 1 - 2 * second}
+        pl.semaphore_signal(barrier, inc=1, device_id=twin, device_id_type=MESH)
+
     loads = [
         pltpu.make_async_copy(ys_ref, y, load_sem.at[0]),
+        pltpu.make_async_copy(idx_hbm, idx_ref, load_sem.at[7]),
         pltpu.make_async_copy(blocks_ref.at[0, pl.ds(REACH * per, per)], kb.at[REACH], load_sem.at[1]),
         pltpu.make_async_copy(xs_ref, x, load_sem.at[2]),
         pltpu.make_async_copy(cost_ref, cost, load_sem.at[3]),
@@ -79,25 +96,6 @@
     ]
     for load in loads:
         load.start()
-
-    barrier = pltpu.get_barrier_semaphore()
-    for offset in OFFSETS:
-        pl.semaphore_signal(
-            barrier, inc=1, device_id={"blk": lax.rem(me + offset + n_dev, n_dev)}, device_id_type=MESH
-        )
-
-    head[pl.ds(scen, head.shape[0] - scen), :] = jnp.zeros((head.shape[0] - scen, width), jnp.float32)
-    for slot in range(SPAN * per):
-        head[pl.ds(scen + slot, 1), :] = jnp.full((1, width), lax.rem(idx_ref[0, slot], per), jnp.float32)
-    loads[0].wait()
-    head[pl.ds(0, scen), :] = y[...].astype(jnp.bfloat16).astype(jnp.float32)
-    ysend[0] = head[...].astype(jnp.bfloat16)
-
-    pl.semaphore_wait(barrier, 2 * REACH)
-
-    heads = {o: remote(ysend.at[0], head_in.at[REACH - o], y_sends.at[0, REACH - o], y_recvs.at[0, REACH - o], o) for o in OFFSETS}
-    for o in OFFSETS:
-        heads[o].start()
     blocks_out = {
         o: remote(
             blocks_ref.at[0, pl.ds((REACH + o) * per, per)],
@@ -108,10 +106,38 @@
         )
         for o in OFFSETS
     }
-    for o in (-1, 1, -2, 2):
-        blocks_out[o].start()
-
-    for load in loads[1:]:
+
+    def send_blocks(offsets):
+        for o in offsets:
+            blocks_out[o].start()
+
+    pl.semaphore_wait(barrier, 2 * REACH + (1 if paired else 0))
+    if paired:
+        pl.when(second == 0)(lambda: send_blocks((-1, 1)))
+    else:
+        send_blocks((-1, 1))
+
+    loads[0].wait()
+    loads[1].wait()
+    head[pl.ds(scen, head.shape[0] - scen), :] = jnp.zeros((head.shape[0] - scen, width), jnp.float32)
+    for slot in range(SPAN * per):
+        head[pl.ds(scen + slot, 1), :] = jnp.full((1, width), lax.rem(idx_ref[0, slot], per), jnp.float32)
+    head[pl.ds(0, scen), :] = y[...].astype(jnp.bfloat16).astype(jnp.float32)
+    ysend[0] = head[...].astype(jnp.bfloat16)
+    heads = {o: remote(ysend.at[0], head_in.at[REACH - o], y_sends.at[0, REACH - o], y_recvs.at[0, REACH - o], o) for o in OFFSETS}
+    for o in OFFSETS:
+        heads[o].start()
+    if paired:
+        pl.when(second == 0)(lambda: send_blocks((-2, 2)))
+
+        @pl.when(second == 1)
+        def _():
+            pl.semaphore_wait(turn, 1)
+            send_blocks((-1, 1, -2, 2))
+    else:
+        send_blocks((-2, 2))
+
+    for load in loads[2:]:
         load.wait()
     bound[...] = cap[...] * jnp.where(dis[...] == 1, 0.25, 1.0)
 
@@ -127,13 +153,18 @@
     for it in range(ITERS):
         last = it == ITERS - 1
         acc = [jnp.broadcast_to(cost[:, pl.ds(c * width, width)], (scen, width)) for c in range(per)]
-        for j in (2, 1, 3, 0, 4):
+        for j in (REACH, 1, 3, 0, 4):
             if j == REACH:
                 low = ysend[it, pl.ds(0, scen), :]
             else:
                 if it == 0:
                     heads[REACH - j].wait_recv()
                     blocks_out[REACH - j].wait_recv()
+                    if paired and j == REACH + 1:
+
+                        @pl.when(second == 0)
+                        def _():
+                            pl.semaphore_signal(turn, inc=1, device_id=twin, device_id_type=MESH)
                     low = head_in[j, pl.ds(0, scen), :]
                 else:
                     remote(ysend.at[it, pl.ds(0, scen)], yin.at[it - 1, j], y_sends.at[it, j], y_recvs.at[it, j], REACH - j).wait_recv()
@@ -173,13 +204,18 @@
             if j == REACH:
                 zown[...] = terms
             else:
-                zsend[it, j] = terms
+                change = (terms if it == 0 else terms - zheld[j]).astype(jnp.bfloat16)
+                zsend[it, j] = change
+                if not last:
+                    zheld[j] = change.astype(jnp.float32) if it == 0 else zheld[j] + change.astype(jnp.float32)
                 remote(zsend.at[it, j], zin.at[it, 2 * REACH - j], z_sends.at[it, j], z_recvs.at[it, 2 * REACH - j], j - REACH).start()
-        total = zown[...]
+        others = jnp.zeros((scen, width), jnp.float32) if it == 0 else zsum[...]
         for j in (1, 3, 0, 4):
             remote(zsend.at[it, j], zin.at[it, j], z_sends.at[it, j], z_recvs.at[it, j], REACH - j).wait_recv()
-            total = total + zin[it, j]
-        new_y = jnp.maximum(y[...] + step_dual * (total - bound[...]), 0.0)
+            others = others + zin[it, j].astype(jnp.float32)
+        if not last:
+            zsum[...] = others
+        new_y = jnp.maximum(y[...] + step_dual * (zown[...] + others - bound[...]), 0.0)
         y[...] = new_y
         if not last:
             ysend[it + 1, pl.ds(0, scen), :] = new_y.astype(jnp.bfloat16)
@@ -205,7 +241,18 @@
     y_store.wait()
 
 
-def per_device(n_dev, blocks, col_index, cost, upper, capacity, disrupted, x_start, y_start):
+def finish(x_in, y_in, x_out, y_out, sems):
+    copies = [
+        pltpu.make_async_copy(x_in, x_out, sems.at[0]),
+        pltpu.make_async_copy(y_in, y_out, sems.at[1]),
+    ]
+    for copy in copies:
+        copy.start()
+    for copy in copies:
+        copy.wait()
+
+
+def per_device(n_dev, paired, blocks, col_index, cost, upper, capacity, disrupted, x_start, y_start):
     slots, width = blocks.shape[1], blocks.shape[3]
     per = slots // SPAN
     scen, ncols = x_start.shape
@@ -213,22 +260,26 @@
     f32, bf16 = jnp.float32, jnp.bfloat16
     anyspace = pl.BlockSpec(memory_space=pl.ANY)
     dma = pltpu.SemaphoreType.DMA
-    return pl.pallas_call(
-        functools.partial(kernel, n_dev),
-        out_shape=(
-            jax.ShapeDtypeStruct(x_start.shape, f32),
-            jax.ShapeDtypeStruct(y_start.shape, f32),
-        ),
-        in_specs=[pl.BlockSpec(memory_space=pltpu.SMEM)] + [anyspace] * 7,
+    shapes = (
+        jax.ShapeDtypeStruct(x_start.shape, f32),
+        jax.ShapeDtypeStruct(y_start.shape, f32),
+    )
+    ends = pl.pallas_call(
+        functools.partial(kernel, n_dev, paired),
+        out_shape=shapes,
+        in_specs=[anyspace] * 8,
         out_specs=(anyspace, anyspace),
         scratch_shapes=[
+            pltpu.SMEM(col_index.shape, jnp.int32),
             pltpu.VMEM((SPAN, per, width, width), bf16),
             pltpu.VMEM((rows_head, width), f32),
             pltpu.VMEM((SPAN, rows_head, width), bf16),
             pltpu.VMEM((ITERS, rows_head, width), bf16),
             pltpu.VMEM((ITERS - 1, SPAN, scen, width), bf16),
-            pltpu.VMEM((ITERS, SPAN, scen, width), f32),
-            pltpu.VMEM((ITERS, SPAN, scen, width), f32),
+            pltpu.VMEM((ITERS, SPAN, scen, width), bf16),
+            pltpu.VMEM((ITERS, SPAN, scen, width), bf16),
+            pltpu.VMEM((scen, width), f32),
+            pltpu.VMEM((SPAN, scen, width), f32),
             pltpu.VMEM((scen, width), f32),
             pltpu.VMEM((scen, ncols), f32),
             pltpu.VMEM((scen, width), f32),
@@ -237,16 +288,17 @@
             pltpu.VMEM((1, width), f32),
             pltpu.VMEM((scen, width), jnp.int32),
             pltpu.VMEM((scen, width), f32),
-            dma((7,)),
+            dma((8,)),
             dma((SPAN,)),
             dma((SPAN,)),
             dma((ITERS, SPAN)),
             dma((ITERS, SPAN)),
             dma((ITERS, SPAN)),
             dma((ITERS, SPAN)),
+            pltpu.SemaphoreType.REGULAR,
         ],
         compiler_params=pltpu.CompilerParams(
-            collective_id=0, has_side_effects=True, vmem_limit_bytes=32 * 1024 * 1024
+            collective_id=0, has_side_effects=True, vmem_limit_bytes=60 * 1024 * 1024
         ),
     )(
         col_index,
@@ -258,6 +310,13 @@
         x_start,
         y_start,
     )
+    return pl.pallas_call(
+        finish,
+        out_shape=shapes,
+        in_specs=[anyspace] * 2,
+        out_specs=(anyspace, anyspace),
+        scratch_shapes=[dma((2,))],
+    )(*ends)
 
 
 def solution(mesh):
@@ -272,7 +331,7 @@
         P("scen", "blk"),
     )
     return jax.shard_map(
-        functools.partial(per_device, mesh.shape["blk"]),
+        functools.partial(per_device, mesh.shape["blk"], mesh.shape["scen"] % 2 == 0),
         mesh=mesh,
         in_specs=placed,
         out_specs=(P("scen", "blk"), P("scen", "blk")),

time: 67.4 us -> 62 us (0.920)
  the two profiles are of different devices: /device:TPU:6 before, /device:TPU:1 now
where the time goes in v2:
time: 62 us; the launch traced here: 61.7 us
  Pallas kernels  61 us (98%)
  between operations  0.64 us (1%)
    pallas_call x1, Pallas kernels, per_device(): pl.pallas_call(functools.partial(kernel, n_dev, paired), out_shape=shapes...  54.9 us
    pallas_call x1, Pallas kernels, per_device(): pl.pallas_call(finish, out_shape=shapes, in_specs=[anyspace] * 2, out_spe...  6.08 us

profile of v2, /device:TPU:1, one launch (start us, length us, event | category | flops | bytes accessed | tf_op | source)
XLA Modules:
  0.0 61.7 jit_solution(7259397005264935781)
XLA Ops:
  0.6 54.9 %shard_map.95 = (f32[64,512]{1,0:T(8,128)}, f32[64,128]{1,0:T(8,128)}) custom-call(s32[1,20]{1,0:T(1,128)} %idx_hbm.1, bf16[1,20,128,128]{3,2,1,0:T(8,128)(2,1)} %blocks_ref.1, f32[1,512]{1,0:T(1,128)} %bitcast.3, f32[1,512]{1,0:T(1,128)} %bitcast.4, f32[1,128]{1,0:T(1,128)} %bitcast.5, s32[64,128]{1,0:T(8,128)} %dis_ref.1, f32[64,512]{1,0:T(8,128)} %xs_ref.1, ...), custom_call_target="tpu_custom_call" | custom-call | tf_op jit(solution)/shard_map/pallas_call | solution.py:267
  55.6 6.1 %shard_map.96 = (f32[64,512]{1,0:T(8,128)}, f32[64,128]{1,0:T(8,128)}) custom-call(f32[64,512]{1,0:T(8,128)} %get-tuple-element.4.x_in, f32[64,128]{1,0:T(8,128)} %get-tuple-element.5.y_in), custom_call_target="tpu_custom_call" | custom-call | tf_op jit(solution)/shard_map/pallas_call | solution.py:313

commit v3 on v2

--- a/solution.py
+++ b/solution.py
@@ -29,8 +29,8 @@
     dis_ref,
     xs_ref,
     ys_ref,
-    x_out,
-    y_out,
+    x,
+    y,
     idx_ref,
     kb,
     head,
@@ -42,8 +42,6 @@
     zown,
     zheld,
     zsum,
-    x,
-    y,
     cost,
     upper,
     cap,
@@ -184,9 +182,6 @@
             new = jnp.minimum(jnp.maximum(old - step_primal * acc[c], 0.0), upper[:, cols])
             bars.append((2.0 * new - old).astype(jnp.bfloat16))
             x[:, cols] = new
-        if last:
-            x_store = pltpu.make_async_copy(x, x_out, load_sem.at[0])
-            x_store.start()
         for j in (0, 4, 1, 3, 2):
             mark = marks(j)
             picked = [bars[0], bars[per - 1]]
@@ -227,8 +222,6 @@
                     y_recvs.at[it + 1, REACH - o],
                     o,
                 ).start()
-    y_store = pltpu.make_async_copy(y, y_out, load_sem.at[1])
-    y_store.start()
     for o in OFFSETS:
         heads[o].wait_send()
         blocks_out[o].wait_send()
@@ -237,19 +230,6 @@
         for it in range(ITERS):
             j = o + REACH
             remote(zsend.at[it, j], zin.at[it, j], z_sends.at[it, j], z_recvs.at[it, j], o).wait_send()
-    x_store.wait()
-    y_store.wait()
-
-
-def finish(x_in, y_in, x_out, y_out, sems):
-    copies = [
-        pltpu.make_async_copy(x_in, x_out, sems.at[0]),
-        pltpu.make_async_copy(y_in, y_out, sems.at[1]),
-    ]
-    for copy in copies:
-        copy.start()
-    for copy in copies:
-        copy.wait()
 
 
 def per_device(n_dev, paired, blocks, col_index, cost, upper, capacity, disrupted, x_start, y_start):
@@ -268,7 +248,7 @@
         functools.partial(kernel, n_dev, paired),
         out_shape=shapes,
         in_specs=[anyspace] * 8,
-        out_specs=(anyspace, anyspace),
+        out_specs=(pl.BlockSpec(memory_space=pltpu.VMEM),) * 2,
         scratch_shapes=[
             pltpu.SMEM(col_index.shape, jnp.int32),
             pltpu.VMEM((SPAN, per, width, width), bf16),
@@ -280,8 +260,6 @@
             pltpu.VMEM((ITERS, SPAN, scen, width), bf16),
             pltpu.VMEM((scen, width), f32),
             pltpu.VMEM((SPAN, scen, width), f32),
-            pltpu.VMEM((scen, width), f32),
-            pltpu.VMEM((scen, ncols), f32),
             pltpu.VMEM((scen, width), f32),
             pltpu.VMEM((1, ncols), f32),
             pltpu.VMEM((1, ncols), f32),
@@ -298,25 +276,24 @@
             pltpu.SemaphoreType.REGULAR,
         ],
         compiler_params=pltpu.CompilerParams(
-            collective_id=0, has_side_effects=True, vmem_limit_bytes=60 * 1024 * 1024
+            collective_id=0, has_side_effects=True, vmem_limit_bytes=32 * 1024 * 1024
         ),
     )(
-        col_index,
-        blocks,
-        cost.reshape(1, -1),
-        upper.reshape(1, -1),
-        capacity.reshape(1, -1),
-        disrupted,
-        x_start,
-        y_start,
+        *(
+            pltpu.with_memory_space_constraint(operand, pltpu.HBM)
+            for operand in (
+                col_index,
+                blocks,
+                cost.reshape(1, -1),
+                upper.reshape(1, -1),
+                capacity.reshape(1, -1),
+                disrupted,
+                x_start,
+                y_start,
+            )
+        )
     )
-    return pl.pallas_call(
-        finish,
-        out_shape=shapes,
-        in_specs=[anyspace] * 2,
-        out_specs=(anyspace, anyspace),
-        scratch_shapes=[dma((2,))],
-    )(*ends)
+    return ends
 
 
 def solution(mesh):

time: 62 us -> 56.6 us (0.913)
  Pallas kernels: 61 us -> 54.4 us
  local copies, waits for them, and re-layouts: 0 us -> 1.27 us
    pallas_call x1 -> x0, Pallas kernels: 6.08 us -> none  [per_device(): pl.pallas_call(finish, out_shape=shapes, in_specs=[anyspace] * 2, out_spe...]
    unnamed x0 -> x2, local copies, waits for them, and re-layouts: none -> 1.27 us
where the time goes in v3:
time: 56.6 us; the launch traced here: 56.3 us
  Pallas kernels  54.4 us (96%)
  local copies, waits for them, and re-layouts  1.27 us (2%)
  between operations  0.64 us (1%)
    pallas_call x1, Pallas kernels, per_device(): pl.pallas_call(functools.partial(kernel, n_dev, paired), out_shape=shapes...  54.4 us
    unnamed x2, local copies, waits for them, and re-layouts  1.27 us

profile of v3, /device:TPU:1, one launch (start us, length us, event | category | flops | bytes accessed | tf_op | source)
XLA Modules:
  0.0 56.3 jit_solution(6296002217597286911)
XLA Ops:
  0.6 54.4 %shard_map.95 = (f32[64,512]{1,0:T(8,128)S(1)}, f32[64,128]{1,0:T(8,128)S(1)}) custom-call(s32[1,20]{1,0:T(1,128)} %idx_hbm.1, bf16[1,20,128,128]{3,2,1,0:T(8,128)(2,1)} %blocks_ref.1, f32[1,512]{1,0:T(1,128)} %bitcast.3, f32[1,512]{1,0:T(1,128)} %bitcast.4, f32[1,128]{1,0:T(1,128)} %bitcast.5, s32[64,128]{1,0:T(8,128)} %dis_ref.1, f32[64,512]{1,0:T(8,128)} %xs_ref.1, ...), custom_call_target="tpu_custom_call" | custom-call | tf_op jit(solution)/shard_map/pallas_call | solution.py:247
  55.0 0.7 %copy.12 = f32[64,512]{1,0:T(8,128)} copy(f32[64,512]{1,0:T(8,128)S(1)} %get-tuple-element.4) | data formatting | bytes 262144
  55.7 0.6 %copy.13 = f32[64,128]{1,0:T(8,128)} copy(f32[64,128]{1,0:T(8,128)S(1)} %get-tuple-element.5) | data formatting | bytes 65536

commit v4 on v3

--- a/solution.py
+++ b/solution.py
@@ -33,6 +33,7 @@
     y,
     idx_ref,
     kb,
+    kt,
     head,
     head_in,
     ysend,
@@ -190,12 +191,13 @@
                 for c in range(1, per):
                     chosen = jnp.where(mark[s] == c, bars[c].astype(jnp.float32), chosen)
                 picked.append(chosen.astype(jnp.bfloat16))
-            terms = lax.dot_general(
-                jnp.concatenate(picked, axis=1),
-                blocks_of(j),
-                (((1,), (1,)), ((), ())),
-                preferred_element_type=jnp.float32,
-            )
+            picked = jnp.concatenate(picked, axis=1)
+            if it == 0:
+                terms = lax.dot_general(
+                    picked, blocks_of(j), (((1,), (1,)), ((), ())), preferred_element_type=jnp.float32
+                )
+            else:
+                terms = jnp.dot(picked, kt[j], preferred_element_type=jnp.float32)
             if j == REACH:
                 zown[...] = terms
             else:
@@ -204,6 +206,10 @@
                 if not last:
                     zheld[j] = change.astype(jnp.float32) if it == 0 else zheld[j] + change.astype(jnp.float32)
                 remote(zsend.at[it, j], zin.at[it, 2 * REACH - j], z_sends.at[it, j], z_recvs.at[it, 2 * REACH - j], j - REACH).start()
+        if it == 0:
+            for j in range(SPAN):
+                for s in range(per):
+                    kt[j, pl.ds(s * width, width), :] = kb[j, s].T
         others = jnp.zeros((scen, width), jnp.float32) if it == 0 else zsum[...]
         for j in (1, 3, 0, 4):
             remote(zsend.at[it, j], zin.at[it, j], z_sends.at[it, j], z_recvs.at[it, j], REACH - j).wait_recv()
@@ -232,6 +238,17 @@
             remote(zsend.at[it, j], zin.at[it, j], z_sends.at[it, j], z_recvs.at[it, j], o).wait_send()
 
 
+def finish(x_in, y_in, x_out, y_out, sems):
+    copies = [
+        pltpu.make_async_copy(x_in, x_out, sems.at[0]),
+        pltpu.make_async_copy(y_in, y_out, sems.at[1]),
+    ]
+    for copy in copies:
+        copy.start()
+    for copy in copies:
+        copy.wait()
+
+
 def per_device(n_dev, paired, blocks, col_index, cost, upper, capacity, disrupted, x_start, y_start):
     slots, width = blocks.shape[1], blocks.shape[3]
     per = slots // SPAN
@@ -252,6 +269,7 @@
         scratch_shapes=[
             pltpu.SMEM(col_index.shape, jnp.int32),
             pltpu.VMEM((SPAN, per, width, width), bf16),
+            pltpu.VMEM((SPAN, per * width, width), bf16),
             pltpu.VMEM((rows_head, width), f32),
             pltpu.VMEM((SPAN, rows_head, width), bf16),
             pltpu.VMEM((ITERS, rows_head, width), bf16),
@@ -293,7 +311,13 @@
             )
         )
     )
-    return ends
+    return pl.pallas_call(
+        finish,
+        out_shape=shapes,
+        in_specs=[anyspace] * 2,
+        out_specs=(anyspace, anyspace),
+        scratch_shapes=[dma((2,))],
+    )(*(pltpu.with_memory_space_constraint(end, pltpu.VMEM) for end in ends))
 
 
 def solution(mesh):

time: 56.6 us -> 56.3 us (level)
  local copies, waits for them, and re-layouts: 1.27 us -> 0 us
  Pallas kernels: 54.4 us -> 55.6 us
    unnamed x2 -> x0, local copies, waits for them, and re-layouts: 1.27 us -> none
    pallas_call x0 -> x1, Pallas kernels: none -> 0.68 us  [per_device(): pl.pallas_call(finish, out_shape=shapes, in_specs=[anyspace] * 2, out_spe...]
where the time goes in v4:
time: 56.3 us; the launch traced here: 56.2 us
  Pallas kernels  55.6 us (99%)
  between operations  0.64 us (1%)
    pallas_call x1, Pallas kernels, per_device(): pl.pallas_call(functools.partial(kernel, n_dev, paired), out_shape=shapes...  54.9 us

profile of v4, /device:TPU:1, one launch (start us, length us, event | category | flops | bytes accessed | tf_op | source)
XLA Modules:
  0.0 56.2 jit_solution(7935502819484684777)
XLA Ops:
  0.6 54.9 %shard_map.95 = (f32[64,512]{1,0:T(8,128)S(1)}, f32[64,128]{1,0:T(8,128)S(1)}) custom-call(s32[1,20]{1,0:T(1,128)} %idx_hbm.1, bf16[1,20,128,128]{3,2,1,0:T(8,128)(2,1)} %blocks_ref.1, f32[1,512]{1,0:T(1,128)} %bitcast.3, f32[1,512]{1,0:T(1,128)} %bitcast.4, f32[1,128]{1,0:T(1,128)} %bitcast.5, s32[64,128]{1,0:T(8,128)} %dis_ref.1, f32[64,512]{1,0:T(8,128)} %xs_ref.1, ...), custom_call_target="tpu_custom_call" | custom-call | tf_op jit(solution)/shard_map/pallas_call | solution.py:264
  55.5 0.7 %shard_map.96 = (f32[64,512]{1,0:T(8,128)}, f32[64,128]{1,0:T(8,128)}) custom-call(f32[64,512]{1,0:T(8,128)S(1)} %get-tuple-element.4.x_in, f32[64,128]{1,0:T(8,128)S(1)} %get-tuple-element.5.y_in), custom_call_target="tpu_custom_call" | custom-call | tf_op jit(solution)/shard_map/pallas_call | solution.py:314

commit v5 on v4

--- a/solution.py
+++ b/solution.py
@@ -152,30 +152,34 @@
     for it in range(ITERS):
         last = it == ITERS - 1
         acc = [jnp.broadcast_to(cost[:, pl.ds(c * width, width)], (scen, width)) for c in range(per)]
-        for j in (REACH, 1, 3, 0, 4):
-            if j == REACH:
-                low = ysend[it, pl.ds(0, scen), :]
-            else:
-                if it == 0:
+        for near in ((REACH,), (1, 3), (0, 4)):
+            for j in near:
+                if j != REACH and it == 0:
                     heads[REACH - j].wait_recv()
                     blocks_out[REACH - j].wait_recv()
-                    if paired and j == REACH + 1:
-
-                        @pl.when(second == 0)
-                        def _():
-                            pl.semaphore_signal(turn, inc=1, device_id=twin, device_id_type=MESH)
+                elif j != REACH:
+                    remote(ysend.at[it, pl.ds(0, scen)], yin.at[it - 1, j], y_sends.at[it, j], y_recvs.at[it, j], REACH - j).wait_recv()
+            if paired and it == 0 and near == (1, 3):
+
+                @pl.when(second == 0)
+                def _():
+                    pl.semaphore_signal(turn, inc=1, device_id=twin, device_id_type=MESH)
+
+            for j in near:
+                if j == REACH:
+                    low = ysend[it, pl.ds(0, scen), :]
+                elif it == 0:
                     low = head_in[j, pl.ds(0, scen), :]
                 else:
-                    remote(ysend.at[it, pl.ds(0, scen)], yin.at[it - 1, j], y_sends.at[it, j], y_recvs.at[it, j], REACH - j).wait_recv()
                     low = yin[it - 1, j]
-            terms = jnp.dot(low, blocks_of(j), preferred_element_type=jnp.float32)
-            acc[0] = acc[0] + terms[:, :width]
-            acc[per - 1] = acc[per - 1] + terms[:, width : 2 * width]
-            mark = marks(j)
-            for s in range(2, per):
-                part = terms[:, s * width : (s + 1) * width]
-                for c in range(per):
-                    acc[c] = acc[c] + jnp.where(mark[s] == c, part, 0.0)
+                terms = jnp.dot(low, blocks_of(j), preferred_element_type=jnp.float32)
+                acc[0] = acc[0] + terms[:, :width]
+                acc[per - 1] = acc[per - 1] + terms[:, width : 2 * width]
+                mark = marks(j)
+                for s in range(2, per):
+                    part = terms[:, s * width : (s + 1) * width]
+                    for c in range(per):
+                        acc[c] = acc[c] + jnp.where(mark[s] == c, part, 0.0)
         bars = []
         for c in range(per):
             cols = pl.ds(c * width, width)
@@ -183,29 +187,35 @@
             new = jnp.minimum(jnp.maximum(old - step_primal * acc[c], 0.0), upper[:, cols])
             bars.append((2.0 * new - old).astype(jnp.bfloat16))
             x[:, cols] = new
-        for j in (0, 4, 1, 3, 2):
-            mark = marks(j)
-            picked = [bars[0], bars[per - 1]]
-            for s in range(2, per):
-                chosen = bars[0].astype(jnp.float32)
-                for c in range(1, per):
-                    chosen = jnp.where(mark[s] == c, bars[c].astype(jnp.float32), chosen)
-                picked.append(chosen.astype(jnp.bfloat16))
-            picked = jnp.concatenate(picked, axis=1)
-            if it == 0:
-                terms = lax.dot_general(
-                    picked, blocks_of(j), (((1,), (1,)), ((), ())), preferred_element_type=jnp.float32
-                )
-            else:
-                terms = jnp.dot(picked, kt[j], preferred_element_type=jnp.float32)
-            if j == REACH:
-                zown[...] = terms
-            else:
-                change = (terms if it == 0 else terms - zheld[j]).astype(jnp.bfloat16)
-                zsend[it, j] = change
-                if not last:
-                    zheld[j] = change.astype(jnp.float32) if it == 0 else zheld[j] + change.astype(jnp.float32)
+        for far in ((0, 4, 1, 3), (REACH,)):
+            terms = {}
+            for j in far:
+                mark = marks(j)
+                picked = [bars[0], bars[per - 1]]
+                for s in range(2, per):
+                    chosen = bars[0].astype(jnp.float32)
+                    for c in range(1, per):
+                        chosen = jnp.where(mark[s] == c, bars[c].astype(jnp.float32), chosen)
+                    picked.append(chosen.astype(jnp.bfloat16))
+                picked = jnp.concatenate(picked, axis=1)
+                if it == 0:
+                    terms[j] = lax.dot_general(
+                        picked, blocks_of(j), (((1,), (1,)), ((), ())), preferred_element_type=jnp.float32
+                    )
+                else:
+                    terms[j] = jnp.dot(picked, kt[j], preferred_element_type=jnp.float32)
+            if far == (REACH,):
+                zown[...] = terms[REACH]
+                continue
+            changes = {}
+            for j in far:
+                changes[j] = (terms[j] if it == 0 else terms[j] - zheld[j]).astype(jnp.bfloat16)
+                zsend[it, j] = changes[j]
+            for j in far:
                 remote(zsend.at[it, j], zin.at[it, 2 * REACH - j], z_sends.at[it, j], z_recvs.at[it, 2 * REACH - j], j - REACH).start()
+            if not last:
+                for j in far:
+                    zheld[j] = changes[j].astype(jnp.float32) if it == 0 else zheld[j] + changes[j].astype(jnp.float32)
         if it == 0:
             for j in range(SPAN):
                 for s in range(per):
@@ -213,11 +223,9 @@
         others = jnp.zeros((scen, width), jnp.float32) if it == 0 else zsum[...]
         for j in (1, 3, 0, 4):
             remote(zsend.at[it, j], zin.at[it, j], z_sends.at[it, j], z_recvs.at[it, j], REACH - j).wait_recv()
+        for j in (1, 3, 0, 4):
             others = others + zin[it, j].astype(jnp.float32)
-        if not last:
-            zsum[...] = others
         new_y = jnp.maximum(y[...] + step_dual * (zown[...] + others - bound[...]), 0.0)
-        y[...] = new_y
         if not last:
             ysend[it + 1, pl.ds(0, scen), :] = new_y.astype(jnp.bfloat16)
             for o in OFFSETS:
@@ -228,6 +236,8 @@
                     y_recvs.at[it + 1, REACH - o],
                     o,
                 ).start()
+            zsum[...] = others
+        y[...] = new_y
     for o in OFFSETS:
         heads[o].wait_send()
         blocks_out[o].wait_send()

time: 56.3 us -> 55.1 us (0.979)
  Pallas kernels: 55.6 us -> 54.2 us
    pallas_call x1, Pallas kernels: 54.9 us -> 53.5 us  [per_device(): pl.pallas_call(functools.partial(kernel, n_dev, paired), out_shape=shapes...]
where the time goes in v5:
time: 55.1 us; the launch traced here: 54.8 us
  Pallas kernels  54.2 us (98%)
  between operations  0.64 us (1%)
    pallas_call x1, Pallas kernels, per_device(): pl.pallas_call(functools.partial(kernel, n_dev, paired), out_shape=shapes...  53.5 us

profile of v5, /device:TPU:1, one launch (start us, length us, event | category | flops | bytes accessed | tf_op | source)
XLA Modules:
  0.0 54.8 jit_solution(14691483372311346964)
XLA Ops:
  0.6 53.5 %shard_map.95 = (f32[64,512]{1,0:T(8,128)S(1)}, f32[64,128]{1,0:T(8,128)S(1)}) custom-call(s32[1,20]{1,0:T(1,128)} %idx_hbm.1, bf16[1,20,128,128]{3,2,1,0:T(8,128)(2,1)} %blocks_ref.1, f32[1,512]{1,0:T(1,128)} %bitcast.3, f32[1,512]{1,0:T(1,128)} %bitcast.4, f32[1,128]{1,0:T(1,128)} %bitcast.5, s32[64,128]{1,0:T(8,128)} %dis_ref.1, f32[64,512]{1,0:T(8,128)} %xs_ref.1, ...), custom_call_target="tpu_custom_call" | custom-call | tf_op jit(solution)/shard_map/pallas_call | solution.py:274
  54.1 0.7 %shard_map.96 = (f32[64,512]{1,0:T(8,128)}, f32[64,128]{1,0:T(8,128)}) custom-call(f32[64,512]{1,0:T(8,128)S(1)} %get-tuple-element.4.x_in, f32[64,128]{1,0:T(8,128)S(1)} %get-tuple-element.5.y_in), custom_call_target="tpu_custom_call" | custom-call | tf_op jit(solution)/shard_map/pallas_call | solution.py:324
